TPU v7x, 32 devices: a whole 2x2x4 slice. The times are simulated.
32 devices in a mesh: tm: 8 (over z, y), stream: 4 (over x, core).
Axes of the slice: x: 2, y: 2, z: 4, core: 2. Of those that a mesh axis runs over, the one named last changes fastest.
Arguments:
- signal: bfloat16 [4, 49152, 256], P('stream', 'tm'), may hold values from -6 to 6
- lengths: int32 [4], P('stream'), may hold values from 12288 to 49152, as said below
- w_conv: bfloat16 [512, 512], replicated, may hold values from -0.25 to 0.25
- w_res: bfloat16 [256, 256], replicated, may hold values from -0.375 to 0.375
- w_in: bfloat16 [256, 1024], replicated, may hold values from -0.375 to 0.375
- w_qkv: bfloat16 [1024, 3072], P(None, 'stream')
- w_out: bfloat16 [1024, 1024], P('stream'), may hold values from -0.1875 to 0.1875
- d_out: bfloat16 [4, 192, 1024], P('stream', 'tm'), may hold values from -6 to 6
Outputs:
- out: bfloat16 [4, 192, 1024], P('stream', 'tm')
- d_signal: bfloat16 [4, 49152, 256], P('stream', 'tm')
- g_conv: float32 [512, 512], P('stream')
- g_res: float32 [256, 256], P('stream')
- g_in: float32 [256, 1024], P('stream')
- g_qkv: float32 [1024, 3072], P('tm', 'stream')
- g_out: float32 [1024, 1024], P('stream', 'tm')
Inputs may be any that keep to these rules, and one draw needn't show every extreme that they name: `lengths`: some stay has all 49152 samples valid and some other stay exactly 12288.
All inputs are finite; a program needn't handle non-finite values.
Results may differ from a plain program's by a relative error of at most 0.013.
Values may be sent and summed in bfloat16 or wider, within the bound.
A program may use at most 128 MiB of HBM per device.

v0:
```python
import functools
import math

import jax
import jax.numpy as jnp
from jax import lax
from jax.experimental import pallas as pl
from jax.experimental.pallas import tpu as pltpu
from jax.sharding import PartitionSpec as P

HEADS = 16
POOL = 256
DILATION_STEP = 512
EPS = 1e-05
BF16 = jnp.bfloat16
F32 = jnp.float32
HIGH = lax.Precision.HIGHEST
MESH = pl.DeviceIdType.MESH
VMEM_SPEC = pl.BlockSpec(memory_space=pltpu.VMEM)


def dot(eq, a, b):
    return jnp.einsum(eq, a, b, preferred_element_type=F32)


def exchange_kernel(axis, n, kinds, *refs):
    k = len(kinds)
    ins, outs = refs[:k], refs[k : 2 * k]
    rest = list(refs[2 * k :])
    slots = [rest.pop(0) if kind.startswith("reduce") or kind == "gatherf" else None for kind in kinds]
    send, recv, local_sem = rest
    me = lax.axis_index(axis)
    barrier = pltpu.get_barrier_semaphore()
    for d in range(1, n):
        pl.semaphore_signal(
            barrier, inc=1, device_id={axis: lax.rem(me + d, n)}, device_id_type=MESH
        )
    pl.semaphore_wait(barrier, n - 1)
    copies = []
    locals_ = []
    for j, kind in enumerate(kinds):
        for d in range(1, n):
            peer = lax.rem(me + d, n)
            src = ins[j] if kind.startswith("gather") else ins[j].at[peer]
            if kind.startswith("reduce"):
                dst = slots[j].at[d - 1]
            elif kind == "gatherf":
                dst = slots[j].at[me]
            elif kind.endswith("1"):
                dst = outs[j].at[:, me]
            else:
                dst = outs[j].at[me]
            copy = pltpu.make_async_remote_copy(
                src_ref=src,
                dst_ref=dst,
                send_sem=send.at[j, d - 1],
                recv_sem=recv.at[j, d - 1],
                device_id={axis: peer},
                device_id_type=MESH,
            )
            copy.start()
            copies.append(copy)
        if not kind.startswith("reduce"):
            src = ins[j] if kind.startswith("gather") else ins[j].at[me]
            land = slots[j] if kind == "gatherf" else outs[j]
            dst = land.at[:, me] if kind.endswith("1") else land.at[me]
            copy = pltpu.make_async_copy(src, dst, local_sem.at[j])
            copy.start()
            locals_.append(copy)
    for copy in locals_:
        copy.wait()
    for copy in copies:
        copy.wait()
    for j, kind in enumerate(kinds):
        if kind.startswith("reduce"):
            total = ins[j][me].astype(F32)
            for d in range(1, n):
                total += slots[j][d - 1].astype(F32)
            outs[j][...] = total.astype(outs[j].dtype)
        elif kind == "gatherf":
            outs[j][...] = slots[j][...].astype(F32)


def exchange(axis, collective, items):
    n = lax.axis_size(axis)
    kinds = tuple(kind for kind, _ in items)
    arrays = [array for _, array in items]
    shapes, slots = [], []
    for kind, array in items:
        inner = array.shape if kind.startswith("gather") else array.shape[1:]
        if kind.startswith("reduce"):
            shapes.append(jax.ShapeDtypeStruct(inner, BF16 if kind == "reduceb" else F32))
            slots.append(pltpu.VMEM((n - 1,) + inner, array.dtype))
        elif kind == "gatherf":
            shapes.append(jax.ShapeDtypeStruct((n,) + inner, F32))
            slots.append(pltpu.VMEM((n,) + inner, array.dtype))
        elif kind.endswith("1"):
            shapes.append(jax.ShapeDtypeStruct((inner[0], n) + inner[1:], array.dtype))
        else:
            shapes.append(jax.ShapeDtypeStruct((n,) + inner, array.dtype))
    k = len(items)
    return pl.pallas_call(
        functools.partial(exchange_kernel, axis, n, kinds),
        out_shape=shapes,
        in_specs=[VMEM_SPEC] * k,
        out_specs=[VMEM_SPEC] * k,
        scratch_shapes=slots
        + [
            pltpu.SemaphoreType.DMA((k, n - 1)),
            pltpu.SemaphoreType.DMA((k, n - 1)),
            pltpu.SemaphoreType.DMA((k,)),
        ],
        compiler_params=pltpu.CompilerParams(collective_id=collective, has_side_effects=True),
        name=f"exchange_{axis}_{collective}",
    )(*arrays)


def attention_kernel(heads, size, scale, len_ref, proj_ref, dctx_ref, ctx_ref, dproj_ref):
    stay = pl.program_id(0)
    total = proj_ref.shape[1]
    length = len_ref[stay]
    row = lax.broadcasted_iota(jnp.int32, (total, total), 0)
    col = lax.broadcasted_iota(jnp.int32, (total, total), 1)
    allowed = (col <= row) & (col * POOL < length)
    nt = (((1,), (1,)), ((), ()))
    tn = (((0,), (0,)), ((), ()))
    for h in range(heads):
        base = h * 3 * size
        query = proj_ref[0, :, base : base + size]
        key = proj_ref[0, :, base + size : base + 2 * size]
        value = proj_ref[0, :, base + 2 * size : base + 3 * size]
        dctx = dctx_ref[0, :, h * size : (h + 1) * size]
        scores = lax.dot_general(query, key, nt, preferred_element_type=F32) * scale
        scores = jnp.where(allowed, scores, -1e30)
        top = jnp.max(scores, axis=-1, keepdims=True)
        weights = jnp.exp(scores - top)
        prob = weights / jnp.sum(weights, axis=-1, keepdims=True)
        prob16 = prob.astype(BF16)
        context = jnp.dot(prob16, value, preferred_element_type=F32)
        ctx_ref[0, :, h * size : (h + 1) * size] = context.astype(BF16)
        d_prob = lax.dot_general(dctx, value, nt, preferred_element_type=F32)
        d_score = prob * (d_prob - jnp.sum(d_prob * prob, axis=-1, keepdims=True))
        d16 = d_score.astype(BF16)
        d_query = scale * jnp.dot(d16, key, preferred_element_type=F32)
        d_key = scale * lax.dot_general(d16, query, tn, preferred_element_type=F32)
        d_value = lax.dot_general(prob16, dctx, tn, preferred_element_type=F32)
        dproj_ref[0, :, base : base + size] = d_query.astype(BF16)
        dproj_ref[0, :, base + size : base + 2 * size] = d_key.astype(BF16)
        dproj_ref[0, :, base + 2 * size : base + 3 * size] = d_value.astype(BF16)


def attention(proj, d_context, group_len, heads, size):
    group, total, width = proj.shape
    inner = heads * size
    wide = pl.BlockSpec((1, total, width), lambda s: (s, 0, 0))
    thin = pl.BlockSpec((1, total, inner), lambda s: (s, 0, 0))
    return pl.pallas_call(
        functools.partial(attention_kernel, heads, size, 1.0 / math.sqrt(size)),
        grid=(group,),
        out_shape=(
            jax.ShapeDtypeStruct((group, total, inner), BF16),
            jax.ShapeDtypeStruct((group, total, width), BF16),
        ),
        in_specs=[pl.BlockSpec(memory_space=pltpu.SMEM), wide, thin],
        out_specs=(thin, wide),
        name="attention",
    )(group_len, proj, d_context)


def riding_copies(axis, kinds, ins, slots, send, recv, keep):
    n = lax.axis_size(axis)
    me = lax.axis_index(axis)
    copies = []
    for j, kind in enumerate(kinds):
        for d in range(1, n):
            peer = lax.rem(me + d, n)
            copies.append(
                pltpu.make_async_remote_copy(
                    src_ref=ins[j] if kind == "gather1" else ins[j].at[peer],
                    dst_ref=slots[j].at[d - 1] if kind == "reduce" else slots[j].at[:, me],
                    send_sem=send.at[j, d - 1],
                    recv_sem=recv.at[j, d - 1],
                    device_id={axis: peer},
                    device_id_type=MESH,
                )
            )
        if kind != "reduce":
            src = ins[j] if kind == "gather1" else ins[j].at[me]
            copies.append(pltpu.make_async_copy(src, slots[j].at[:, me], keep.at[j]))
    return copies


def ride_start(axis, kinds, ins, slots, send, recv, keep):
    n = lax.axis_size(axis)
    me = lax.axis_index(axis)
    barrier = pltpu.get_barrier_semaphore()
    for d in range(1, n):
        pl.semaphore_signal(
            barrier, inc=1, device_id={axis: lax.rem(me + d, n)}, device_id_type=MESH
        )
    pl.semaphore_wait(barrier, n - 1)
    for copy in riding_copies(axis, kinds, ins, slots, send, recv, keep):
        copy.start()


def ride_finish(axis, kinds, ins, outs, slots, send, recv, keep):
    n = lax.axis_size(axis)
    me = lax.axis_index(axis)
    for copy in riding_copies(axis, kinds, ins, slots, send, recv, keep):
        copy.wait()
    for j, kind in enumerate(kinds):
        if kind == "reduce":
            sum_ = ins[j][me].astype(F32)
            for d in range(1, n):
                sum_ += slots[j][d - 1].astype(F32)
            outs[j][...] = sum_
        else:
            outs[j][...] = slots[j][...]


def ride_shapes(n, items):
    shapes, scratch = [], []
    for kind, array in items:
        inner = array.shape if kind == "gather1" else array.shape[1:]
        if kind == "reduce":
            shapes.append(jax.ShapeDtypeStruct(inner, F32))
            scratch.append(pltpu.VMEM((n - 1,) + inner, array.dtype))
        else:
            out = (inner[0], n) + inner[1:]
            shapes.append(jax.ShapeDtypeStruct(out, array.dtype))
            scratch.append(pltpu.VMEM(out, array.dtype))
    k = len(items)
    sems = [pltpu.SemaphoreType.DMA((k, n - 1))] * 2 + [pltpu.SemaphoreType.DMA((k,))]
    specs = [pl.BlockSpec(a.shape, functools.partial(origin, a.ndim)) for _, a in items]
    outs = [pl.BlockSpec(a.shape, functools.partial(origin, len(a.shape))) for a in shapes]
    return shapes, scratch + sems, specs, outs


def origin(rank, i):
    return (0,) * rank


def tile_valid(info_ref, tile, step):
    row = lax.broadcasted_iota(jnp.int32, (tile, 1), 0)
    return info_ref[0] + step * tile + row < info_ref[1]


def joined_tile(first, in_ref, past_ref, cur_ref):
    past = jnp.where(first, in_ref[...], past_ref[...])
    return jnp.concatenate([past, cur_ref[...]], axis=1)


def forward_kernel(
    steps, axis, kinds, info_ref, in_ref, past_ref, cur_ref, w_ref, *refs
):
    k = len(kinds)
    ins, (t_ref, s_ref, hs_ref, ss_ref) = refs[:k], refs[k : k + 4]
    outs, slots, sems = refs[k + 4 : 2 * k + 4], refs[2 * k + 4 : 3 * k + 4], refs[3 * k + 4 :]
    i = pl.program_id(0)

    @pl.when(i == 0)
    def _():
        ride_start(axis, kinds, ins, slots, *sems)

    tile, chans = cur_ref.shape
    joined = joined_tile(i == 0, in_ref, past_ref, cur_ref)
    mixed = jnp.dot(joined, w_ref[...], preferred_element_type=F32)
    t = jnp.tanh(mixed[:, :chans])
    s = jax.nn.sigmoid(mixed[:, chans:])
    t_ref[...] = t
    s_ref[...] = s
    valid = tile_valid(info_ref, tile, i)
    hidden = jnp.where(valid, (t * s).astype(BF16).astype(F32), 0.0)
    kept = jnp.where(valid, cur_ref[...].astype(F32), 0.0)
    for j in range(tile // POOL):
        rows = slice(j * POOL, (j + 1) * POOL)
        hs_ref[0, j : j + 1, :] = jnp.sum(hidden[rows], axis=0, keepdims=True)
        ss_ref[0, j : j + 1, :] = jnp.sum(kept[rows], axis=0, keepdims=True)

    @pl.when(i == steps - 1)
    def _():
        ride_finish(axis, kinds, ins, outs, slots, *sems)


def backward_kernel(
    steps, axis, kinds, info_ref, in_ref, past_ref, cur_ref, t_ref, s_ref, dh_ref, dr_ref, w_ref,
    *refs,
):
    k = len(kinds)
    ins, (sig_ref, first_ref, g_ref) = refs[:k], refs[k : k + 3]
    outs, (acc_ref, later_ref) = refs[k + 3 : 2 * k + 3], refs[2 * k + 3 : 2 * k + 5]
    slots, sems = refs[2 * k + 5 : 3 * k + 5], refs[3 * k + 5 :]
    i = pl.program_id(0)

    @pl.when(i == 0)
    def _():
        ride_start(axis, kinds, ins, slots, *sems)

    step = steps - 1 - i
    tile, chans = cur_ref.shape

    @pl.when(i == 0)
    def _():
        acc_ref[...] = jnp.zeros_like(acc_ref)
        later_ref[...] = jnp.zeros_like(later_ref)

    joined = joined_tile(step == 0, in_ref, past_ref, cur_ref)
    valid = tile_valid(info_ref, tile, step)

    def spread(ref):
        pieces = [
            jnp.broadcast_to(ref[0, j : j + 1, :], (POOL, chans)) for j in range(tile // POOL)
        ]
        return jnp.where(valid, jnp.concatenate(pieces, axis=0), 0.0)

    t, s = t_ref[...], s_ref[...]
    d_hidden = spread(dh_ref)
    d_gate = d_hidden * s
    d_mixed = jnp.concatenate(
        [d_gate * (1.0 - t * t), d_gate * t * (1.0 - s)], axis=1
    ).astype(BF16)
    acc_ref[...] += lax.dot_general(
        joined, d_mixed, (((0,), (0,)), ((), ())), preferred_element_type=F32
    )
    d_joined = lax.dot_general(
        d_mixed, w_ref[...], (((1,), (1,)), ((), ())), preferred_element_type=F32
    )
    sig_ref[...] = (spread(dr_ref) + d_joined[:, chans:] + later_ref[...].astype(F32)).astype(BF16)
    later_ref[...] = d_joined[:, :chans].astype(BF16)

    @pl.when(i == steps - 1)
    def _():
        first_ref[...] = d_joined[:, :chans].astype(BF16)
        g_ref[...] = acc_ref[...].astype(BF16)
        ride_finish(axis, kinds, ins, outs, slots, *sems)


def final_kernel(axis, n, *refs):
    ins, outs, slots, mine, lands = refs[:3], refs[3:6], refs[6:8], refs[8:10], refs[10:13]
    send, recv, keep = refs[13:]
    me = lax.axis_index(axis)
    barrier = pltpu.get_barrier_semaphore()
    for d in range(1, n):
        pl.semaphore_signal(
            barrier, inc=1, device_id={axis: lax.rem(me + d, n)}, device_id_type=MESH
        )
    pl.semaphore_wait(barrier, n - 1)

    def push(row, d, src, dst):
        copy = pltpu.make_async_remote_copy(
            src_ref=src,
            dst_ref=dst,
            send_sem=send.at[row, d - 1],
            recv_sem=recv.at[row, d - 1],
            device_id={axis: lax.rem(me + d, n)},
            device_id_type=MESH,
        )
        copy.start()
        return copy

    parts = [
        push(j, d, ins[j].at[lax.rem(me + d, n)], slots[j].at[d - 1])
        for j in range(2)
        for d in range(1, n)
    ]
    rest = [push(2, d, ins[2], lands[2].at[me]) for d in range(1, n)]
    for copy in parts:
        copy.wait()
    for j in range(2):
        total = ins[j][me].astype(F32)
        for d in range(1, n):
            total += slots[j][d - 1].astype(F32)
        mine[j][...] = total.astype(BF16)
    for j, src in enumerate((mine[0], mine[1], ins[2])):
        copy = pltpu.make_async_copy(src, lands[j].at[me], keep.at[j])
        copy.start()
        rest.append(copy)
    rest += [push(3 + j, d, mine[j], lands[j].at[me]) for j in range(2) for d in range(1, n)]
    for copy in rest:
        copy.wait()
    for j in range(3):
        outs[j][...] = lands[j][...].astype(F32)


def final_sums(axis, collective, conv, res, cols):
    n = lax.axis_size(axis)
    shapes = [conv.shape, res.shape, (n,) + cols.shape]
    sums = [conv.shape[1:], res.shape[1:]]
    return pl.pallas_call(
        functools.partial(final_kernel, axis, n),
        out_shape=[jax.ShapeDtypeStruct(a, F32) for a in shapes],
        in_specs=[VMEM_SPEC] * 3,
        out_specs=[VMEM_SPEC] * 3,
        scratch_shapes=[pltpu.VMEM((n - 1,) + a, BF16) for a in sums]
        + [pltpu.VMEM(a, BF16) for a in sums]
        + [pltpu.VMEM(a, BF16) for a in shapes]
        + [pltpu.SemaphoreType.DMA((5, n - 1))] * 2
        + [pltpu.SemaphoreType.DMA((3,))],
        compiler_params=pltpu.CompilerParams(collective_id=collective, has_side_effects=True),
        name="final_sums",
    )(conv, res, cols)


def conv_forward(info, incoming, signal, w_conv, axis, collective, items):
    kinds = tuple(kind for kind, _ in items)
    shapes, scratch, specs, out_specs = ride_shapes(lax.axis_size(axis), items)
    samples, chans = signal.shape
    tile = DILATION_STEP
    steps, pools = samples // tile, tile // POOL
    block = pl.BlockSpec((tile, chans), lambda i: (i, 0))
    sums = pl.BlockSpec((1, pools, chans), lambda i: (i, 0, 0))
    gate = jax.ShapeDtypeStruct((samples, chans), F32)
    pooled = jax.ShapeDtypeStruct((steps, pools, chans), F32)
    return pl.pallas_call(
        functools.partial(forward_kernel, steps, axis, kinds),
        grid=(steps,),
        out_shape=[gate, gate, pooled, pooled] + shapes,
        in_specs=[
            pl.BlockSpec(memory_space=pltpu.SMEM),
            pl.BlockSpec((tile, chans), lambda i: (0, 0)),
            pl.BlockSpec((tile, chans), lambda i: (jnp.maximum(i - 1, 0), 0)),
            block,
            pl.BlockSpec(w_conv.shape, lambda i: (0, 0)),
        ]
        + specs,
        out_specs=[block, block, sums, sums] + out_specs,
        scratch_shapes=scratch,
        compiler_params=pltpu.CompilerParams(collective_id=collective, has_side_effects=True),
        name="conv_forward",
    )(info, incoming, signal, signal, w_conv, *[array for _, array in items])


def conv_backward(
    info, incoming, signal, t, s, d_hidden, d_resid, w_conv, axis, collective, items
):
    kinds = tuple(kind for kind, _ in items)
    shapes, scratch, specs, out_specs = ride_shapes(lax.axis_size(axis), items)
    samples, chans = signal.shape
    tile = DILATION_STEP
    steps, pools = samples // tile, tile // POOL
    block = pl.BlockSpec((tile, chans), lambda i: (steps - 1 - i, 0))
    fixed = pl.BlockSpec((tile, chans), lambda i: (0, 0))
    sums = pl.BlockSpec((1, pools, chans), lambda i: (steps - 1 - i, 0, 0))
    whole = pl.BlockSpec(w_conv.shape, lambda i: (0, 0))
    return pl.pallas_call(
        functools.partial(backward_kernel, steps, axis, kinds),
        grid=(steps,),
        out_shape=[
            jax.ShapeDtypeStruct((samples, chans), BF16),
            jax.ShapeDtypeStruct((tile, chans), BF16),
            jax.ShapeDtypeStruct(w_conv.shape, BF16),
        ]
        + shapes,
        in_specs=[
            pl.BlockSpec(memory_space=pltpu.SMEM),
            fixed,
            pl.BlockSpec((tile, chans), lambda i: (jnp.maximum(steps - 2 - i, 0), 0)),
            block,
            block,
            block,
            sums,
            sums,
            whole,
        ]
        + specs,
        out_specs=[block, fixed, whole] + out_specs,
        scratch_shapes=[pltpu.VMEM(w_conv.shape, F32), pltpu.VMEM((tile, chans), BF16)] + scratch,
        compiler_params=pltpu.CompilerParams(collective_id=collective, has_side_effects=True),
        name="conv_backward",
    )(info, incoming, signal, signal, t, s, d_hidden, d_resid, w_conv, *[a for _, a in items])


def shifted(value, axis, by):
    length = lax.axis_size(axis)
    pairs = [(i, i + by) for i in range(length) if 0 <= i + by < length]
    return lax.ppermute(value, axis, pairs)


def local(signal, lengths, w_conv, w_res, w_in, w_qkv, w_out, d_out):
    stays, samples, chans = signal.shape
    width = w_in.shape[1]
    size = width // HEADS
    heads = w_out.shape[0] // size
    toks = samples // POOL
    tms, parts = lax.axis_size("tm"), lax.axis_size("stream")
    tm = lax.axis_index("tm")
    group = stays * parts
    total = toks * tms
    flat = signal.reshape(samples, chans)
    incoming = shifted(flat[samples - DILATION_STEP :], "tm", 1)
    info = jnp.stack([tm * samples, lengths[0]]).astype(jnp.int32)
    lens8 = jnp.broadcast_to(lengths.reshape(stays, 1, 1), (stays, 8, 128))
    g_dout, g_len = exchange("stream", 0, [("gather", d_out), ("gather", lens8)])
    group_grad = g_dout.reshape(group, toks, width)
    group_len = g_len.reshape(group, 8, 128)[:, 0, 0]
    d_ctx = dot("btd,ed->bte", group_grad, w_out).astype(BF16)
    columns = width // tms
    grad_cols = group_grad.reshape(group, toks, tms, columns).transpose(2, 0, 1, 3)
    tanh_f, sig_g, h_sum, s_sum, all_ctx, all_cols = conv_forward(
        info, incoming, flat, w_conv, "tm", 6, [("gather1", d_ctx), ("scatter1", grad_cols)]
    )
    h_sum = h_sum.reshape(toks, chans)
    h_part = jnp.dot(h_sum, w_res.astype(F32), precision=HIGH)
    pooled = ((s_sum.reshape(toks, chans) + h_part) / POOL).astype(BF16)[None]
    own_tok = dot("btc,cd->btd", pooled, w_in).astype(BF16)
    (stay_pool,) = exchange("tm", 1, [("gather1", pooled)])
    (all_pool,) = exchange("stream", 7, [("gather", stay_pool.reshape(stays, total, chans))])
    all_pool = all_pool.reshape(group, total, chans)
    all_ctx = all_ctx.reshape(group, total, heads * size)
    all_cols = all_cols.reshape(group, total, columns)
    tok = dot("btc,cd->btd", all_pool, w_in).astype(BF16).astype(F32)
    r = lax.rsqrt(jnp.mean(tok * tok, axis=-1, keepdims=True) + EPS)
    normed = (tok * r).astype(BF16)
    proj = dot("btd,de->bte", normed, w_qkv).astype(BF16)
    context, d_proj = attention(proj, all_ctx, group_len, heads, size)
    own_ctx = lax.dynamic_slice_in_dim(context, tm * toks, toks, 1)
    out_part = dot("bte,ed->btd", own_ctx, w_out).astype(BF16)
    g_out = dot("bte,btd->ed", context, all_cols)
    own_norm = lax.dynamic_slice_in_dim(normed, tm * columns, columns, 2)
    g_qkv = dot("btd,bte->de", own_norm, d_proj)
    d_normed = dot("bte,de->btd", d_proj, w_qkv)
    inner = jnp.sum(d_normed * tok, axis=-1, keepdims=True)
    d_group = (r * d_normed - tok * (r * r * r) * inner / width).astype(BF16)
    own_group = lax.dynamic_slice_in_dim(d_group, tm * toks, toks, 1)
    g_in_part = dot("btc,btd->cd", all_pool, d_group).astype(BF16)
    in_rows = chans // parts
    g_in_cols = dot("btc,btd->cd", all_pool, all_cols)
    stream = lax.axis_index("stream")
    g_in_cols = lax.dynamic_slice_in_dim(g_in_cols, stream * in_rows, in_rows, 0)
    (s_group,) = exchange(
        "stream", 2, [("reduce", own_group.reshape(parts, stays, toks, width))]
    )
    d_tok = (s_group + d_out.astype(F32)).astype(BF16)
    d_pooled = dot("btd,cd->btc", d_tok, w_in)
    d_res16 = (d_pooled / POOL).astype(BF16).reshape(toks, chans)
    g_res = lax.dot_general(h_sum, d_res16.astype(F32), (((0,), (0,)), ((), ())), precision=HIGH)
    d_hidden = lax.dot_general(
        d_res16, w_res, (((1,), (1,)), ((), ())), preferred_element_type=F32
    )
    per_tile = (samples // DILATION_STEP, DILATION_STEP // POOL, chans)
    d_sig, first, g_conv, s_out, s_in = conv_backward(
        info,
        incoming,
        flat,
        tanh_f,
        sig_g,
        d_hidden.reshape(per_tile),
        d_res16.astype(F32).reshape(per_tile),
        w_conv,
        "stream",
        8,
        [
            ("reduce", out_part.reshape(parts, stays, toks, width)),
            ("reduce", g_in_part.reshape(parts, in_rows, width)),
        ],
    )
    out = (own_tok.astype(F32) + s_out).astype(BF16)
    arriving = shifted(first, "tm", -1)
    edge = samples - DILATION_STEP
    last = (d_sig[edge:].astype(F32) + arriving.astype(F32)).astype(BF16)
    d_signal = jnp.concatenate([d_sig[:edge], last], axis=0)[None]
    s_conv, s_res = exchange(
        "stream",
        3,
        [
            ("reduceb", g_conv.reshape(parts, -1, 2 * chans)),
            ("reduceb", g_res.astype(BF16).reshape(parts, -1, chans)),
        ],
    )
    a_conv, a_res, a_in = final_sums(
        "tm",
        4,
        s_conv.reshape(tms, -1, 2 * chans),
        s_res.reshape(tms, -1, chans),
        g_in_cols.astype(BF16),
    )
    sum_conv = a_conv.reshape(2 * chans // parts, 2 * chans).astype(F32)
    sum_res = a_res.reshape(chans // parts, chans).astype(F32)
    sum_in = s_in + a_in.transpose(1, 0, 2).reshape(in_rows, width).astype(F32)
    return (out, d_signal, sum_conv, sum_res, sum_in, g_qkv, g_out)


def solution(mesh):
    in_specs = (
        P("stream", "tm", None),
        P("stream"),
        P(),
        P(),
        P(),
        P(None, "stream"),
        P("stream", None),
        P("stream", "tm", None),
    )
    out_specs = (
        P("stream", "tm", None),
        P("stream", "tm", None),
        P("stream", None),
        P("stream", None),
        P("stream", None),
        P("tm", "stream"),
        P("stream", "tm"),
    )
    return jax.shard_map(local, mesh=mesh, in_specs=in_specs, out_specs=out_specs, check_vma=False)
```

profile of v0, /device:TPU:0, one launch (start us, length us, event | category | flops | bytes accessed | tf_op | source)
XLA Modules:
  0.0 167.7 jit_solution(13160960879089267762)
XLA Ops:
  0.6 0.0 copy-start
  0.6 1.1 slice_bitcast_fusion
  1.7 4.9 %collective-permute-start = (bf16[512,256]{1,0:T(8,128)(2,1)S(1)}, bf16[512,256]{1,0:T(8,128)(2,1)S(1)}, u32[]{:S(2)}, u32[]{:S(2)}) collective-permute-start(bf16[512,256]{1,0:T(8,128)(2,1)S(1)} %slice_bitcast_fusion), channel_id=1, source_target_pairs={{0,4},{4,8},{8,12},{12,16},{16,20},{20,24},{24,28},{1,5},{5,9},{9,... | collective-permute-start | bytes 786440 | tf_op jit(solution)/shard_map/ppermute | solution.py:476
  7.3 0.6 broadcast_in_dim.16.refs_1_
  7.9 6.8 %exchange_stream_0.1 = (bf16[4,1,24,1024]{3,2,1,0:T(8,128)(2,1)}, s32[4,1,8,128]{3,2,1,0:T(8,128)}) custom-call(bf16[1,24,1024]{2,1,0:T(8,128)(2,1)} %refs_0_.1, s32[1,8,128]{2,1,0:T(8,128)} %broadcast_in_dim.16.refs_1_), custom_call_target="tpu_custom_call" | custom-call | tf_op jit(solution)/shard_map/exchange_stream_0/pallas_call | solution.py:102
  14.8 1.4 slice_reduce_fusion.len_ref
  16.2 0.6 pad_add_fusion.info_ref
  16.7 1.0 copy.22
  17.7 0.7 copy.27
  18.4 2.1 %convolution_convert_fusion.3.refs_0_ = bf16[4,24,256]{2,1,0:T(8,128)(2,1)} fusion(bf16[256,1024]{1,0:T(8,128)(2,1)} %param.14, bf16[4,1,24,1024]{3,2,1,0:T(8,128)(2,1)} %get-tuple-element.27), kind=kOutput, calls=%fused_computation.27 | convolution fusion | flops 50356224 | bytes 770048 | tf_op jit(solution)/shard_map/btd,ed->bte/dot_general | solution.py:23
  20.5 0.7 copy-done.8
  21.2 20.0 %conv_forward.1 = (f32[6144,256]{1,0:T(8,128)}, f32[6144,256]{1,0:T(8,128)}, f32[12,2,256]{2,1,0:T(2,128)}, f32[12,2,256]{2,1,0:T(2,128)}, bf16[4,8,24,256]{3,2,...) custom-call(s32[2]{0:T(128)} %pad_add_fusion.info_ref, bf16[512,256]{1,0:T(8,128)(2,1)} %copy-done.8, ...), custom_call_target="tpu_custom_call" | custom-call | tf_op jit(solution)/shard_map/conv_forward/pallas_call | solution.py:414
  41.2 0.8 reshape.113
  42.0 0.8 reshape.114
  42.7 0.2 fusion.36
  42.9 0.6 multiply_convert_fusion
  43.5 8.7 %exchange_tm_1.1 = bf16[1,8,24,256]{3,2,1,0:T(8,128)(2,1)} custom-call(bf16[1,24,256]{2,1,0:T(8,128)(2,1)} %bitcast.118), custom_call_target="tpu_custom_call" | custom-call | tf_op jit(solution)/shard_map/exchange_tm_1/pallas_call | solution.py:102
  52.3 7.9 %exchange_stream_7.1 = bf16[4,1,192,256]{3,2,1,0:T(8,128)(2,1)} custom-call(bf16[1,192,256]{2,1,0:T(8,128)(2,1)} %bitcast.115), custom_call_target="tpu_custom_call" | custom-call | tf_op jit(solution)/shard_map/exchange_stream_7/pallas_call | solution.py:102
  60.2 2.0 %convolution_bitcast_fusion.3 = bf16[256,128]{1,0:T(8,128)(2,1)} fusion(bf16[4,192,128]{2,1,0:T(8,128)(2,1)} %bitcast.108, bf16[4,1,192,256]{3,2,1,0:T(8,128)(2,1)} %exchange_stream_7.1), kind=kOutput, calls=%fused_computation.26 | convolution fusion | flops 50331648 | bytes 655360 | tf_op jit(solution)/shard_map/btc,btd->cd/dot_general | solution.py:23
  62.2 1.7 fusion.1
  63.9 0.3 fusion.2
  64.3 2.4 %fusion.12.proj_ref = bf16[4,192,768]{2,1,0:T(8,128)(2,1)} fusion(bf16[4,192,1024]{2,1,0:T(8,128)(2,1)S(1)} %fusion.2, bf16[1024,768]{1,0:T(8,128)(2,1)S(1)} %copy-done), kind=kOutput, calls=%fused_computation.18 | convolution fusion | flops 1208549376 | bytes 4325376 | tf_op jit(solution)/shard_map/btd,de->bte/dot_general | solution.py:23
  66.7 12.5 %attention.1 = (bf16[4,192,256]{2,1,0:T(8,128)(2,1)}, bf16[4,192,768]{2,1,0:T(8,128)(2,1)}) custom-call(s32[4]{0:T(128)} %slice_reduce_fusion.len_ref, bf16[4,192,768]{2,1,0:T(8,128)(2,1)} %fusion.12.proj_ref, bf16[4,192,256]{2,1,0:T(8,128)(2,1)} %bitcast.114), custom_call_target="tpu_custom_call" | custom-call | tf_op jit(solution)/shard_map/attention/pallas_call | solution.py:157
  79.2 2.0 %convolution_bitcast_fusion.2 = f32[256,128]{1,0:T(8,128)} fusion(bf16[4,192,256]{2,1,0:T(8,128)(2,1)} %get-tuple-element.35, bf16[4,192,128]{2,1,0:T(8,128)(2,1)S(1)} %bitcast.109), kind=kOutput, calls=%fused_computation.25 | convolution fusion | flops 50331648 | bytes 720896 | tf_op jit(solution)/shard_map/bte,btd->ed/dot_general | solution.py:23
  81.2 1.7 %fusion.16.refs_0_ = bf16[4,1,24,1024]{3,2,1,0:T(8,128)(2,1)} fusion(bf16[256,1024]{1,0:T(8,128)(2,1)S(1)} %copy-done.1, bf16[4,192,256]{2,1,0:T(8,128)(2,1)} %get-tuple-element.35, s32[]{:T(128)S(6)} %select_n.10), kind=kOutput, calls=%fused_computation.23 | convolution fusion | flops 50429952 | bytes 770052 | tf_op jit(solution)/shard_map/bte,ed->btd/dot_general | solution.py:23
  82.9 2.8 %fusion.8 = f32[4,192,1024]{2,1,0:T(8,128)S(1)} fusion(bf16[4,192,768]{2,1,0:T(8,128)(2,1)} %get-tuple-element.34, bf16[1024,768]{1,0:T(8,128)(2,1)S(1)} %copy-done), kind=kOutput, calls=%fused_computation.14 | convolution fusion | flops 1207959552 | bytes 5898240 | tf_op jit(solution)/shard_map/bte,de->btd/dot_general | solution.py:23
  85.7 1.5 fusion.6
  87.3 1.4 fusion.15
  88.7 0.7 dynamic-slice_bitcast_fusion.refs_0_
  89.3 6.6 %exchange_stream_2.1 = f32[1,24,1024]{2,1,0:T(8,128)} custom-call(bf16[4,1,24,1024]{3,2,1,0:T(8,128)(2,1)} %dynamic-slice_bitcast_fusion.refs_0_), custom_call_target="tpu_custom_call" | custom-call | tf_op jit(solution)/shard_map/exchange_stream_2/pallas_call | solution.py:102
  96.0 1.1 fusion.19
  97.2 0.6 convert_element_type.84.dr_ref
  97.8 0.1 fusion.28
  97.9 1.0 convolution_convert_fusion.2
  99.0 2.0 %convolution_bitcast_fusion.1 = f32[128,768]{1,0:T(8,128)} fusion(bf16[4,192,768]{2,1,0:T(8,128)(2,1)S(1)} %copy-done.7, bf16[4,192,1024]{2,1,0:T(8,128)(2,1)} %copy-done.3, s32[]{:T(128)S(6)} %select_n.12), kind=kOutput, calls=%fused_computation.21 | convolution fusion | flops 150994944 | bytes 1769476 | tf_op jit(solution)/shard_map/btd,bte->de/dot_general | solution.py:23
  101.0 0.6 copy.19.dh_ref
  101.6 18.7 %conv_backward.1 = (bf16[6144,256]{1,0:T(8,128)(2,1)}, bf16[512,256]{1,0:T(8,128)(2,1)}, bf16[512,512]{1,0:T(8,128)(2,1)}, f32[1,24,1024]{2,1,0:T(8,128)}, f32[64,1024]{1,0:T(8,128)}) custom-call(s32[2]{0:T(128)} %pad_add_fusion.info_ref, bf16[512,256]{1,0:T(8,128)(2,1)} %copy-done.8, bf16[6144,256]{1,0:T(8,128)(2,1)} %bitcast.104, ...), custom_call_target="tpu_custom_call" | custom-call | tf_op jit(solution)/shard_map/conv_backward/pallas_call | solution.py:445
  120.4 1.7 %add_convert_fusion.1 = bf16[1,24,1024]{2,1,0:T(8,128)(2,1)} fusion(f32[1,24,1024]{2,1,0:T(8,128)} %get-tuple-element.36, bf16[24,256]{1,0:T(8,128)(2,1)S(1)} %copy-done.15, bf16[256,1024]{1,0:T(8,128)(2,1)S(1)} %copy-done.2), kind=kOutput, calls=%fused_computation.48 | convolution fusion | flops 12681216 | bytes 684032 | tf_op jit(solution)/shard_map/btc,cd->btd/dot_general | solution.py:23
  122.1 1.3 collective-permute-start.1
  123.4 1.3 dynamic-slice_convert_fusion.refs_2_
  124.7 3.6 %slice.18 = bf16[5632,256]{1,0:T(8,128)(2,1)} slice(bf16[6144,256]{1,0:T(8,128)(2,1)} %get-tuple-element.37), slice={[0:5632], [0:256]} | slice | bytes 5767168 | tf_op jit(solution)/shard_map/slice | solution.py:561
  128.3 11.6 %exchange_stream_3.1 = (bf16[128,512]{1,0:T(8,128)(2,1)}, bf16[64,256]{1,0:T(8,128)(2,1)}) custom-call(bf16[4,128,512]{2,1,0:T(8,128)(2,1)} %bitcast.112, bf16[4,64,256]{2,1,0:T(8,128)(2,1)} %bitcast.113), custom_call_target="tpu_custom_call" | custom-call | tf_op jit(solution)/shard_map/exchange_stream_3/pallas_call | solution.py:102
  139.9 20.0 %final_sums.1 = (f32[8,16,512]{2,1,0:T(8,128)}, f32[8,8,256]{2,1,0:T(8,128)}, f32[8,64,128]{2,1,0:T(8,128)}) custom-call(bf16[8,16,512]{2,1,0:T(8,128)(2,1)} %bitcast.117, bf16[8,8,256]{2,1,0:T(8,128)(2,1)} %bitcast.120, bf16[64,128]{1,0:T(8,128)(2,1)} %dynamic-slice_convert_fusion.refs_2_), custom_call_target="tpu_custom_call" | custom-call | tf_op jit(solution)/shard_map/final_sums/pallas_call | solution.py:389
  159.9 1.7 %bitcast_add_fusion = f32[64,1024]{1,0:T(8,128)} fusion(f32[64,1024]{1,0:T(8,128)S(1)} %copy-done.12, f32[8,64,128]{2,1,0:T(8,128)} %get-tuple-element.46), kind=kLoop, calls=%fused_computation.40 | loop fusion | flops 65536 | bytes 786432 | tf_op jit(solution)/shard_map/add | solution.py:579
  161.6 1.0 add_convert_fusion
  162.6 3.7 %maximum_bitcast_fusion = bf16[1,6144,256]{2,1,0:T(8,128)(2,1)} fusion(bf16[512,256]{1,0:T(8,128)(2,1)S(1)} %add_convert_fusion, bf16[5632,256]{1,0:T(8,128)(2,1)} %slice.18), kind=kLoop, calls=%fused_computation.11 | loop fusion | flops 6291456 | bytes 6291456 | tf_op jit(solution)/shard_map/broadcast_in_dim | solution.py:561
  166.3 0.7 copy.31
  167.0 0.6 copy.32
  (36 shorter events, 0.1 us)
Async XLA Ops:
  0.6 63.6 %copy-start = (bf16[1024,768]{1,0:T(8,128)(2,1)S(1)}, bf16[1024,768]{1,0:T(8,128)(2,1)}, u32[]{:S(2)}) copy-start(bf16[1024,768]{1,0:T(8,128)(2,1)} %param.13) | copy-start | bytes 4718596
  1.7 18.8 %collective-permute-start = (bf16[512,256]{1,0:T(8,128)(2,1)S(1)}, bf16[512,256]{1,0:T(8,128)(2,1)S(1)}, u32[]{:S(2)}, u32[]{:S(2)}) collective-permute-start(bf16[512,256]{1,0:T(8,128)(2,1)S(1)} %slice_bitcast_fusion), channel_id=1, source_target_pairs={{0,4},{4,8},{8,12},{12,16},{16,20},{20,24},{24,28},{1,5},{5,9},{9,... | collective-permute-start | bytes 786440 | tf_op jit(solution)/shard_map/ppermute | solution.py:476
  20.5 0.7 copy-start.8
  21.2 21.5 %copy-start.10 = (bf16[256,256]{1,0:T(8,128)(2,1)S(1)}, bf16[256,256]{1,0:T(8,128)(2,1)}, u32[]{:S(2)}) copy-start(bf16[256,256]{1,0:T(8,128)(2,1)} %param.11) | copy-start | bytes 393220
  21.2 41.0 %copy-start.2 = (bf16[256,1024]{1,0:T(8,128)(2,1)S(1)}, bf16[256,1024]{1,0:T(8,128)(2,1)}, u32[]{:S(2)}) copy-start(bf16[256,1024]{1,0:T(8,128)(2,1)} %param.12) | copy-start | bytes 1572868
  63.9 2.8 %copy-start.4 = (bf16[4,192,1024]{2,1,0:T(8,128)(2,1)}, bf16[4,192,1024]{2,1,0:T(8,128)(2,1)S(1)}, u32[]{:S(2)}) copy-start(bf16[4,192,1024]{2,1,0:T(8,128)(2,1)S(1)} %get-tuple-element.50) | copy-start | bytes 4718596
  64.2 2.5 %copy-start.3 = (bf16[4,192,1024]{2,1,0:T(8,128)(2,1)}, bf16[4,192,1024]{2,1,0:T(8,128)(2,1)S(1)}, u32[]{:S(2)}) copy-start(bf16[4,192,1024]{2,1,0:T(8,128)(2,1)S(1)} %fusion.2) | copy-start | bytes 4718596
  64.3 14.9 %copy-start.9 = (bf16[4,8,24,128]{3,2,1,0:T(8,128)(2,1)S(1)}, bf16[4,8,24,128]{3,2,1,0:T(8,128)(2,1)}, u32[]{:S(2)}) copy-start(bf16[4,8,24,128]{3,2,1,0:T(8,128)(2,1)} %get-tuple-element.42) | copy-start | bytes 589828
  64.3 16.9 %copy-start.1 = (bf16[256,1024]{1,0:T(8,128)(2,1)S(1)}, bf16[256,1024]{1,0:T(8,128)(2,1)}, u32[]{:S(2)}) copy-start(bf16[256,1024]{1,0:T(8,128)(2,1)} %param.14) | copy-start | bytes 1572868
  82.9 2.8 %copy-start.5 = (bf16[4,192,1024]{2,1,0:T(8,128)(2,1)S(1)}, bf16[4,192,1024]{2,1,0:T(8,128)(2,1)}, u32[]{:S(2)}) copy-start(bf16[4,192,1024]{2,1,0:T(8,128)(2,1)} %copy-done.4) | copy-start | bytes 4718596
  85.7 1.5 copy-start.6
  87.2 8.8 %copy-start.14 = (bf16[1,24,1024]{2,1,0:T(8,128)(2,1)S(1)}, bf16[1,24,1024]{2,1,0:T(8,128)(2,1)}, u32[]{:S(2)}) copy-start(bf16[1,24,1024]{2,1,0:T(8,128)(2,1)} %refs_0_.1) | copy-start | bytes 147460
  87.2 10.6 %copy-start.11 = (bf16[256,256]{1,0:T(8,128)(2,1)S(1)}, bf16[256,256]{1,0:T(8,128)(2,1)}, u32[]{:S(2)}) copy-start(bf16[256,256]{1,0:T(8,128)(2,1)} %param.11) | copy-start | bytes 393220
  87.2 11.7 %copy-start.7 = (bf16[4,192,768]{2,1,0:T(8,128)(2,1)S(1)}, bf16[4,192,768]{2,1,0:T(8,128)(2,1)}, u32[]{:S(2)}) copy-start(bf16[4,192,768]{2,1,0:T(8,128)(2,1)} %get-tuple-element.34) | copy-start | bytes 3538948
  101.6 18.7 %copy-start.15 = (bf16[24,256]{1,0:T(8,128)(2,1)S(1)}, bf16[24,256]{1,0:T(8,128)(2,1)}, u32[]{:S(2)}) copy-start(bf16[24,256]{1,0:T(8,128)(2,1)} %multiply_convert_fusion) | copy-start | bytes 36868
  122.1 39.5 %collective-permute-start.1 = (bf16[512,256]{1,0:T(8,128)(2,1)}, bf16[512,256]{1,0:T(8,128)(2,1)S(1)}, u32[]{:S(2)}, u32[]{:S(2)}) collective-permute-start(bf16[512,256]{1,0:T(8,128)(2,1)} %get-tuple-element.38), channel_id=1, source_target_pairs={{4,0},{8,4},{12,8},{16,12},{20,16},{24,20},{28,24},{5,1},{9,5},{13... | collective-permute-start | bytes 786440 | tf_op jit(solution)/shard_map/ppermute | solution.py:476
  124.7 35.2 %copy-start.12 = (f32[64,1024]{1,0:T(8,128)S(1)}, f32[64,1024]{1,0:T(8,128)}, u32[]{:S(2)}) copy-start(f32[64,1024]{1,0:T(8,128)} %get-tuple-element.45) | copy-start | bytes 786436
  162.6 3.7 %copy-start.13 = (f32[8,16,512]{2,1,0:T(8,128)S(1)}, f32[8,16,512]{2,1,0:T(8,128)}, u32[]{:S(2)}) copy-start(f32[8,16,512]{2,1,0:T(8,128)} %get-tuple-element.43) | copy-start | bytes 786436
  162.6 4.4 %copy-start.16 = (f32[8,8,256]{2,1,0:T(8,128)S(1)}, f32[8,8,256]{2,1,0:T(8,128)}, u32[]{:S(2)}) copy-start(f32[8,8,256]{2,1,0:T(8,128)} %get-tuple-element.44) | copy-start | bytes 196612
where the time goes:
time: 169 us; the launch traced here: 168 us
  Pallas kernels  113 us (67%)
  matrix products  22.2 us (13%)
  local copies, waits for them, and re-layouts  14.7 us (9%)
  other arithmetic  10.1 us (6%)
  starting transfers between devices  6.2 us (4%)
    pallas_call x5, Pallas kernels, exchange(): pl.pallas_call(functools.partial(exchange_kernel, axis, n, kinds), out_sh...  41.7 us
    dot_general x11, matrix products, dot(): return jnp.einsum(eq, a, b, preferred_element_type=F32)  20.9 us
    pallas_call x1, Pallas kernels, conv_forward(): pl.pallas_call(functools.partial(forward_kernel, steps, axis, kinds), gri...  20 us
    pallas_call x1, Pallas kernels, final_sums(): pl.pallas_call(functools.partial(final_kernel, axis, n), out_shape=[jax.S...  20 us
    pallas_call x1, Pallas kernels, conv_backward(): pl.pallas_call(functools.partial(backward_kernel, steps, axis, kinds), gr...  18.7 us
    pallas_call x1, Pallas kernels, attention(): pl.pallas_call(functools.partial(attention_kernel, heads, size, 1.0 / mat...  12.5 us
    ppermute x2, starting transfers between devices, shifted(): return lax.ppermute(value, axis, pairs)  6.2 us
    broadcast_in_dim x1, other arithmetic, local(): d_signal = jnp.concatenate([d_sig[:edge], last], axis=0)[None]  3.73 us
  transfers between devices with their start and end apart: 2, of which 0 were waited for; matrix products, arithmetic and copies ran while one was open for 8% of the time, Pallas kernels for 23%

commit v1 on v0

--- a/solution.py
+++ b/solution.py
@@ -250,40 +250,8 @@
     return jnp.concatenate([past, cur_ref[...]], axis=1)
 
 
-def forward_kernel(
-    steps, axis, kinds, info_ref, in_ref, past_ref, cur_ref, w_ref, *refs
-):
-    k = len(kinds)
-    ins, (t_ref, s_ref, hs_ref, ss_ref) = refs[:k], refs[k : k + 4]
-    outs, slots, sems = refs[k + 4 : 2 * k + 4], refs[2 * k + 4 : 3 * k + 4], refs[3 * k + 4 :]
-    i = pl.program_id(0)
-
-    @pl.when(i == 0)
-    def _():
-        ride_start(axis, kinds, ins, slots, *sems)
-
-    tile, chans = cur_ref.shape
-    joined = joined_tile(i == 0, in_ref, past_ref, cur_ref)
-    mixed = jnp.dot(joined, w_ref[...], preferred_element_type=F32)
-    t = jnp.tanh(mixed[:, :chans])
-    s = jax.nn.sigmoid(mixed[:, chans:])
-    t_ref[...] = t
-    s_ref[...] = s
-    valid = tile_valid(info_ref, tile, i)
-    hidden = jnp.where(valid, (t * s).astype(BF16).astype(F32), 0.0)
-    kept = jnp.where(valid, cur_ref[...].astype(F32), 0.0)
-    for j in range(tile // POOL):
-        rows = slice(j * POOL, (j + 1) * POOL)
-        hs_ref[0, j : j + 1, :] = jnp.sum(hidden[rows], axis=0, keepdims=True)
-        ss_ref[0, j : j + 1, :] = jnp.sum(kept[rows], axis=0, keepdims=True)
-
-    @pl.when(i == steps - 1)
-    def _():
-        ride_finish(axis, kinds, ins, outs, slots, *sems)
-
-
 def backward_kernel(
-    steps, axis, kinds, info_ref, in_ref, past_ref, cur_ref, t_ref, s_ref, dh_ref, dr_ref, w_ref,
+    steps, axis, kinds, info_ref, in_ref, past_ref, cur_ref, a_ref, dh_ref, dr_ref, w_ref,
     *refs,
 ):
     k = len(kinds)
@@ -313,11 +281,9 @@
         ]
         return jnp.where(valid, jnp.concatenate(pieces, axis=0), 0.0)
 
-    t, s = t_ref[...], s_ref[...]
     d_hidden = spread(dh_ref)
-    d_gate = d_hidden * s
-    d_mixed = jnp.concatenate(
-        [d_gate * (1.0 - t * t), d_gate * t * (1.0 - s)], axis=1
+    d_mixed = (
+        a_ref[...].astype(F32) * jnp.concatenate([d_hidden, d_hidden], axis=1)
     ).astype(BF16)
     acc_ref[...] += lax.dot_general(
         joined, d_mixed, (((0,), (0,)), ((), ())), preferred_element_type=F32
@@ -401,37 +367,8 @@
     )(conv, res, cols)
 
 
-def conv_forward(info, incoming, signal, w_conv, axis, collective, items):
-    kinds = tuple(kind for kind, _ in items)
-    shapes, scratch, specs, out_specs = ride_shapes(lax.axis_size(axis), items)
-    samples, chans = signal.shape
-    tile = DILATION_STEP
-    steps, pools = samples // tile, tile // POOL
-    block = pl.BlockSpec((tile, chans), lambda i: (i, 0))
-    sums = pl.BlockSpec((1, pools, chans), lambda i: (i, 0, 0))
-    gate = jax.ShapeDtypeStruct((samples, chans), F32)
-    pooled = jax.ShapeDtypeStruct((steps, pools, chans), F32)
-    return pl.pallas_call(
-        functools.partial(forward_kernel, steps, axis, kinds),
-        grid=(steps,),
-        out_shape=[gate, gate, pooled, pooled] + shapes,
-        in_specs=[
-            pl.BlockSpec(memory_space=pltpu.SMEM),
-            pl.BlockSpec((tile, chans), lambda i: (0, 0)),
-            pl.BlockSpec((tile, chans), lambda i: (jnp.maximum(i - 1, 0), 0)),
-            block,
-            pl.BlockSpec(w_conv.shape, lambda i: (0, 0)),
-        ]
-        + specs,
-        out_specs=[block, block, sums, sums] + out_specs,
-        scratch_shapes=scratch,
-        compiler_params=pltpu.CompilerParams(collective_id=collective, has_side_effects=True),
-        name="conv_forward",
-    )(info, incoming, signal, signal, w_conv, *[array for _, array in items])
-
-
 def conv_backward(
-    info, incoming, signal, t, s, d_hidden, d_resid, w_conv, axis, collective, items
+    info, incoming, signal, gates, d_hidden, d_resid, w_conv, axis, collective, items
 ):
     kinds = tuple(kind for kind, _ in items)
     shapes, scratch, specs, out_specs = ride_shapes(lax.axis_size(axis), items)
@@ -456,8 +393,7 @@
             fixed,
             pl.BlockSpec((tile, chans), lambda i: (jnp.maximum(steps - 2 - i, 0), 0)),
             block,
-            block,
-            block,
+            pl.BlockSpec((tile, 2 * chans), lambda i: (steps - 1 - i, 0)),
             sums,
             sums,
             whole,
@@ -467,7 +403,308 @@
         scratch_shapes=[pltpu.VMEM(w_conv.shape, F32), pltpu.VMEM((tile, chans), BF16)] + scratch,
         compiler_params=pltpu.CompilerParams(collective_id=collective, has_side_effects=True),
         name="conv_backward",
-    )(info, incoming, signal, signal, t, s, d_hidden, d_resid, w_conv, *[a for _, a in items])
+    )(info, incoming, signal, signal, gates, d_hidden, d_resid, w_conv, *[a for _, a in items])
+
+
+def device_of(tm, stream):
+    return {"tm": tm, "stream": stream}
+
+
+def front_kernel(
+    steps, group, len_ref, sig_hbm, w_ref, wout_ref, wres_ref, wgrad_ref,
+    a_hbm, edge_hbm, hsum_ref, pool_ref, ctx_ref, cols_ref, lens_ref,
+    sig, a_buf, grads, gate_w, ctx_mine, cols_mine, sums, sem_in, sem_out, send_tm, recv_tm,
+    send_st, recv_st, send_pool, recv_pool, send_near, recv_near, keep,
+):
+    tms, parts = lax.axis_size("tm"), lax.axis_size("stream")
+    tm, st = lax.axis_index("tm"), lax.axis_index("stream")
+    chips = parts // 2
+    core, chip = lax.rem(st, 2), st // 2
+    mine = tm * chips + chip
+    tile = DILATION_STEP
+    samples = steps * tile
+    chans = w_ref.shape[1] // 2
+    toks = samples // POOL
+    rounds = steps // group
+
+    def peer_of(flat):
+        return device_of(flat // chips, lax.rem(flat, chips) * 2 + core)
+
+    barrier = pltpu.get_barrier_semaphore()
+
+    def greet(device):
+        pl.semaphore_signal(barrier, inc=1, device_id=device, device_id_type=MESH)
+
+    others = tms * chips
+    lax.fori_loop(1, others, lambda d, c: (greet(peer_of(lax.rem(mine + d, others))), c)[1], 0)
+    for d in range(chips):
+        greet(device_of(tm, lax.rem(chip + d, chips) * 2 + 1 - core))
+
+    def load(i):
+        return pltpu.make_async_copy(
+            sig_hbm.at[pl.ds(i * tile, tile)], sig.at[pl.ds((i + 1) * tile, tile)], sem_in.at[i]
+        )
+
+    def save(i):
+        return pltpu.make_async_copy(
+            a_buf.at[pl.ds(i * tile, tile)], a_hbm.at[pl.ds(i * tile, tile)], sem_out.at[i]
+        )
+
+    for i in reversed(range(steps)):
+        load(i).start()
+    gate_w[...] = w_ref[:, chans:] * jnp.asarray(0.5, BF16)
+
+    halo = pltpu.make_async_remote_copy(
+        src_ref=sig_hbm.at[pl.ds(samples - tile, tile)],
+        dst_ref=sig.at[pl.ds(0, tile)],
+        send_sem=send_tm.at[2, 0],
+        recv_sem=recv_tm.at[2, 0],
+        device_id={"tm": lax.rem(tm + 1, tms)},
+        device_id_type=MESH,
+    )
+
+    def to_stream(j, d, src, dst):
+        return pltpu.make_async_remote_copy(
+            src_ref=src,
+            dst_ref=dst,
+            send_sem=send_st.at[j, d - 1],
+            recv_sem=recv_st.at[j, d - 1],
+            device_id={"stream": lax.rem(st + d, parts)},
+            device_id_type=MESH,
+        )
+
+    grad_copies = [
+        copy
+        for d in range(1, parts)
+        for copy in (
+            to_stream(0, d, wgrad_ref, grads.at[st]),
+            to_stream(1, d, lens_ref.at[st], lens_ref.at[st]),
+        )
+    ]
+
+    def to_tm(j, d, src, dst):
+        return pltpu.make_async_remote_copy(
+            src_ref=src,
+            dst_ref=dst,
+            send_sem=send_tm.at[j, d - 1],
+            recv_sem=recv_tm.at[j, d - 1],
+            device_id={"tm": lax.rem(tm + d, tms)},
+            device_id_type=MESH,
+        )
+
+    width = grads.shape[2]
+    columns = width // tms
+
+    tm_copies = [
+        copy
+        for d in range(1, tms)
+        for copy in (
+            to_tm(0, d, ctx_mine, ctx_ref.at[tm]),
+            to_tm(1, d, cols_mine.at[lax.rem(tm + d, tms)], cols_ref.at[tm]),
+        )
+    ]
+    own_grad = pltpu.make_async_copy(wgrad_ref, grads.at[st], keep.at[0])
+    own_ctx = pltpu.make_async_copy(ctx_mine, ctx_ref.at[tm], keep.at[1])
+    own_cols = pltpu.make_async_copy(cols_mine.at[tm], cols_ref.at[tm], keep.at[2])
+    edge = pltpu.make_async_copy(sig.at[pl.ds(0, tile)], edge_hbm, keep.at[3])
+
+    lens_ref[st] = jnp.full(lens_ref.shape[1:], len_ref[0], jnp.int32)
+    length = len_ref[0]
+
+    def chunk(token):
+        base = token * POOL
+        past = sig[pl.ds(base, POOL), :]
+        cur = sig[pl.ds(base + tile, POOL), :]
+        mixed_f = jnp.dot(past, w_ref[:chans, :chans], preferred_element_type=F32)
+        mixed_f += jnp.dot(cur, w_ref[chans:, :chans], preferred_element_type=F32)
+        mixed_g = jnp.dot(past, gate_w[:chans], preferred_element_type=F32)
+        mixed_g += jnp.dot(cur, gate_w[chans:], preferred_element_type=F32)
+        row = lax.broadcasted_iota(jnp.int32, (POOL, 128), 0) + (tm * samples + base)
+        half = jnp.where(row < length, 0.5, 0.0)
+        half = jnp.concatenate([half] * (chans // 128), axis=1)
+        t = jnp.tanh(mixed_f)
+        s = half * jnp.tanh(mixed_g) + half
+        h = t * s
+        a_buf[pl.ds(base, POOL), :chans] = (s - t * h).astype(BF16)
+        a_buf[pl.ds(base, POOL), chans:] = (h - h * s).astype(BF16)
+        hs = jnp.sum(h, axis=0, keepdims=True)
+        ss = jnp.sum(cur.astype(F32) * half, axis=0, keepdims=True) * 2.0
+        return hs, ss
+
+    def body(it, carry):
+        r = rounds - 1 - it
+        per_tile = tile // POOL
+        rows = [None] * (group * per_tile)
+        for k in reversed(range(group)):
+            i = r * group + k
+            if k > 0:
+                load(i - 1).wait()
+            else:
+
+                @pl.when(r > 0)
+                def _():
+                    load(i - 1).wait()
+
+                @pl.when((r == 0) & (tm > 0))
+                def _():
+                    halo.wait_recv()
+
+                @pl.when((r == 0) & (tm == 0))
+                def _():
+                    sig[pl.ds(0, tile), :] = jnp.zeros((tile, chans), BF16)
+
+            for j in range(per_tile):
+                rows[k * per_tile + j] = chunk(i * per_tile + j)
+            save(i).start()
+        block = pl.ds(pl.multiple_of(r * group * per_tile, 8), group * per_tile)
+        hsum_ref[block, :] = jnp.concatenate([a for a, _ in rows], axis=0)
+        sums[block, :] = jnp.concatenate([b for _, b in rows], axis=0)
+
+        @pl.when(it == 0)
+        def _():
+            pl.semaphore_wait(barrier, others - 1 + chips)
+
+            @pl.when(tm < tms - 1)
+            def _():
+                halo.start()
+            own_grad.start()
+            for copy in grad_copies:
+                copy.start()
+
+        @pl.when(it == 1)
+        def _():
+            own_grad.wait()
+            for copy in grad_copies:
+                copy.wait()
+            for p in range(parts):
+                ctx_mine[p] = lax.dot_general(
+                    grads[p], wout_ref[...], (((1,), (1,)), ((), ())), preferred_element_type=F32
+                ).astype(BF16)
+                for k in range(tms):
+                    cols_mine[k, p] = grads[p, :, k * columns : (k + 1) * columns]
+            own_ctx.start()
+            own_cols.start()
+            for copy in tm_copies:
+                copy.start()
+
+        return carry
+
+    load(steps - 1).wait()
+    lax.fori_loop(0, rounds, body, 0)
+    edge.start()
+
+    total = hsum_ref[...]
+    high = total.astype(BF16)
+    low = (total - high.astype(F32)).astype(BF16)
+    resid = jnp.dot(high, wres_ref[...], preferred_element_type=F32)
+    resid += jnp.dot(low, wres_ref[...], preferred_element_type=F32)
+    pool_ref[st, tm] = ((sums[...] + resid) / POOL).astype(BF16)
+
+    def spread(d):
+        return pltpu.make_async_remote_copy(
+            src_ref=pool_ref.at[st, tm],
+            dst_ref=pool_ref.at[st, tm],
+            send_sem=send_pool.at[d],
+            recv_sem=recv_pool.at[d],
+            device_id=peer_of(lax.rem(mine + d, others)),
+            device_id_type=MESH,
+        )
+
+    def relay(d):
+        flat = lax.rem(mine - d + others, others)
+        block = pool_ref.at[lax.rem(flat, chips) * 2 + core, flat // chips]
+        return pltpu.make_async_remote_copy(
+            src_ref=block,
+            dst_ref=block,
+            send_sem=send_near.at[d],
+            recv_sem=recv_near.at[d],
+            device_id={"stream": chip * 2 + 1 - core},
+            device_id_type=MESH,
+        )
+
+    def launch(d, c):
+        spread(d).start()
+        return c
+
+    def forward(d, c):
+        spread(d).wait_recv()
+        relay(d).start()
+        return c
+
+    def settle(d, c):
+        spread(d).wait_send()
+        return c
+
+    def close(d, c):
+        relay(d).wait()
+        return c
+
+    lax.fori_loop(1, others, launch, 0)
+    relay(0).start()
+    lax.fori_loop(1, others, forward, 0)
+    for copy in tm_copies:
+        copy.wait()
+    own_ctx.wait()
+    own_cols.wait()
+    edge.wait()
+    for i in range(steps):
+        save(i).wait()
+
+    @pl.when(tm < tms - 1)
+    def _():
+        halo.wait_send()
+
+    lax.fori_loop(1, others, settle, 0)
+    lax.fori_loop(0, others, close, 0)
+
+
+def front(lengths, signal, w_conv, w_out, w_res, d_out, collective):
+    samples, chans = signal.shape
+    toks, width = d_out.shape
+    tms, parts = lax.axis_size("tm"), lax.axis_size("stream")
+    steps = samples // DILATION_STEP
+    group = 4
+    inner = w_out.shape[0]
+    others = tms * parts // 2
+    columns = width // tms
+    anywhere = pl.BlockSpec(memory_space=pl.ANY)
+    dma = pltpu.SemaphoreType.DMA
+    return pl.pallas_call(
+        functools.partial(front_kernel, steps, group),
+        out_shape=[
+            jax.ShapeDtypeStruct((samples, 2 * chans), BF16),
+            jax.ShapeDtypeStruct((DILATION_STEP, chans), BF16),
+            jax.ShapeDtypeStruct((toks, chans), F32),
+            jax.ShapeDtypeStruct((parts, tms, toks, chans), BF16),
+            jax.ShapeDtypeStruct((tms, parts, toks, inner), BF16),
+            jax.ShapeDtypeStruct((tms, parts, toks, columns), BF16),
+            jax.ShapeDtypeStruct((parts, 8, 128), jnp.int32),
+        ],
+        in_specs=[pl.BlockSpec(memory_space=pltpu.SMEM), anywhere] + [VMEM_SPEC] * 4,
+        out_specs=[anywhere, anywhere] + [VMEM_SPEC] * 5,
+        scratch_shapes=[
+            pltpu.VMEM((samples + DILATION_STEP, chans), BF16),
+            pltpu.VMEM((samples, 2 * chans), BF16),
+            pltpu.VMEM((parts, toks, width), BF16),
+            pltpu.VMEM((2 * chans, chans), BF16),
+            pltpu.VMEM((parts, toks, inner), BF16),
+            pltpu.VMEM((tms, parts, toks, columns), BF16),
+            pltpu.VMEM((toks, chans), F32),
+            dma((steps,)),
+            dma((steps,)),
+            dma((3, tms - 1)),
+            dma((3, tms - 1)),
+            dma((2, parts - 1)),
+            dma((2, parts - 1)),
+            dma((others,)),
+            dma((others,)),
+            dma((others,)),
+            dma((others,)),
+            dma((4,)),
+        ],
+        compiler_params=pltpu.CompilerParams(collective_id=collective, has_side_effects=True),
+        name="front",
+    )(lengths, signal, w_conv, w_out, w_res, d_out)
 
 
 def shifted(value, axis, by):
@@ -487,27 +724,18 @@
     group = stays * parts
     total = toks * tms
     flat = signal.reshape(samples, chans)
-    incoming = shifted(flat[samples - DILATION_STEP :], "tm", 1)
     info = jnp.stack([tm * samples, lengths[0]]).astype(jnp.int32)
-    lens8 = jnp.broadcast_to(lengths.reshape(stays, 1, 1), (stays, 8, 128))
-    g_dout, g_len = exchange("stream", 0, [("gather", d_out), ("gather", lens8)])
-    group_grad = g_dout.reshape(group, toks, width)
-    group_len = g_len.reshape(group, 8, 128)[:, 0, 0]
-    d_ctx = dot("btd,ed->bte", group_grad, w_out).astype(BF16)
     columns = width // tms
-    grad_cols = group_grad.reshape(group, toks, tms, columns).transpose(2, 0, 1, 3)
-    tanh_f, sig_g, h_sum, s_sum, all_ctx, all_cols = conv_forward(
-        info, incoming, flat, w_conv, "tm", 6, [("gather1", d_ctx), ("scatter1", grad_cols)]
-    )
-    h_sum = h_sum.reshape(toks, chans)
-    h_part = jnp.dot(h_sum, w_res.astype(F32), precision=HIGH)
-    pooled = ((s_sum.reshape(toks, chans) + h_part) / POOL).astype(BF16)[None]
-    own_tok = dot("btc,cd->btd", pooled, w_in).astype(BF16)
-    (stay_pool,) = exchange("tm", 1, [("gather1", pooled)])
-    (all_pool,) = exchange("stream", 7, [("gather", stay_pool.reshape(stays, total, chans))])
+    gates, incoming, h_sum, all_pool, all_ctx, all_cols, lens = front(
+        lengths, flat, w_conv, w_out, w_res, d_out.reshape(toks, width), 0
+    )
+    group_len = lens[:, 0, 0]
+    own_pool = lax.dynamic_slice_in_dim(all_pool, tm, 1, 1)
+    own_pool = lax.dynamic_slice_in_dim(own_pool, lax.axis_index("stream"), 1, 0)
+    own_tok = dot("btc,cd->btd", own_pool.reshape(1, toks, chans), w_in).astype(BF16)
     all_pool = all_pool.reshape(group, total, chans)
-    all_ctx = all_ctx.reshape(group, total, heads * size)
-    all_cols = all_cols.reshape(group, total, columns)
+    all_ctx = all_ctx.transpose(1, 0, 2, 3).reshape(group, total, heads * size)
+    all_cols = all_cols.transpose(1, 0, 2, 3).reshape(group, total, columns)
     tok = dot("btc,cd->btd", all_pool, w_in).astype(BF16).astype(F32)
     r = lax.rsqrt(jnp.mean(tok * tok, axis=-1, keepdims=True) + EPS)
     normed = (tok * r).astype(BF16)
@@ -542,8 +770,7 @@
         info,
         incoming,
         flat,
-        tanh_f,
-        sig_g,
+        gates,
         d_hidden.reshape(per_tile),
         d_res16.astype(F32).reshape(per_tile),
         w_conv,

time: 169 us -> 150 us (0.89)
  Pallas kernels: 113 us -> 102 us
  starting transfers between devices: 6.2 us -> 1.42 us
    pallas_call x5 -> x2, Pallas kernels: 41.7 us -> 17.8 us  [exchange(): pl.pallas_call(functools.partial(exchange_kernel, axis, n, kinds), out_sh...]
    pallas_call x1, Pallas kernels: 20 us -> 34.2 us  [front(): pl.pallas_call(functools.partial(front_kernel, steps, group), out_shape=[...]
    ppermute x2 -> x1, starting transfers between devices: 6.2 us -> 1.42 us  [shifted(): return lax.ppermute(value, axis, pairs)]
    transpose x0 -> x2, local copies, waits for them, and re-layouts: none -> 2.71 us  [the longest x1 1.77 us: local(): all_ctx = all_ctx.transpose(1, 0, 2, 3).reshape(group, total, heads * size)]
    dot_general x11 -> x10, matrix products: 20.9 us -> 18.9 us  [dot(): return jnp.einsum(eq, a, b, preferred_element_type=F32)]
  transfers between devices with their start and end apart: 2 -> 1, of which waited for: 0 -> 0; matrix products, arithmetic and copies ran while one was open for 8% -> 11% of each run, Pallas kernels for 23% -> 21%
where the time goes in v1:
time: 150 us; the launch traced here: 149 us
  Pallas kernels  102 us (68%)
  matrix products  20.7 us (14%)
  local copies, waits for them, and re-layouts  13.9 us (9%)
  other arithmetic  9.49 us (6%)
  between operations  1.65 us (1%)
    pallas_call x1, Pallas kernels, front(): pl.pallas_call(functools.partial(front_kernel, steps, group), out_shape=[...  34.2 us
    pallas_call x1, Pallas kernels, final_sums(): pl.pallas_call(functools.partial(final_kernel, axis, n), out_shape=[jax.S...  19.7 us
    dot_general x10, matrix products, dot(): return jnp.einsum(eq, a, b, preferred_element_type=F32)  18.9 us
    pallas_call x2, Pallas kernels, exchange(): pl.pallas_call(functools.partial(exchange_kernel, axis, n, kinds), out_sh...  17.8 us
    pallas_call x1, Pallas kernels, conv_backward(): pl.pallas_call(functools.partial(backward_kernel, steps, axis, kinds), gr...  17.4 us
    pallas_call x1, Pallas kernels, attention(): pl.pallas_call(functools.partial(attention_kernel, heads, size, 1.0 / mat...  12.5 us
    broadcast_in_dim x1, other arithmetic, local(): d_signal = jnp.concatenate([d_sig[:edge], last], axis=0)[None]  3.73 us
    slice x1, local copies, waits for them, and re-layouts, local(): d_signal = jnp.concatenate([d_sig[:edge], last], axis=0)[None]  3.64 us
  transfers between devices with their start and end apart: 1, of which 0 were waited for; matrix products, arithmetic and copies ran while one was open for 11% of the time, Pallas kernels for 21%

profile of v1, /device:TPU:0, one launch (start us, length us, event | category | flops | bytes accessed | tf_op | source)
XLA Modules:
  0.0 148.7 jit_solution(17369060655998303327)
XLA Ops:
  0.6 0.0 copy-start
  0.6 0.0 copy-start.2
  1.5 34.2 %front.1 = (bf16[6144,512]{1,0:T(8,128)(2,1)}, bf16[512,256]{1,0:T(8,128)(2,1)}, f32[24,256]{1,0:T(8,128)}, bf16[4,8,24,256]{3,2,1,0:T(8,128)(2,1)}, bf16[8,4,24...) custom-call(s32[1]{0:T(128)S(6)} %copy.34.len_ref, bf16[6144,256]{1,0:T(8,128)(2,1)} %bitcast.88, ...), custom_call_target="tpu_custom_call" | custom-call | tf_op jit(solution)/shard_map/front/pallas_call | solution.py:672
  35.7 1.4 slice_reduce_fusion.len_ref
  37.1 1.8 %copy.19 = bf16[4,8,24,256]{3,2,1,0:T(8,128)(2,1)} copy(bf16[4,8,24,256]{3,2,0,1:T(8,128)(2,1)} %bitcast.96) | data formatting | bytes 786432 | tf_op jit(solution)/shard_map/transpose | solution.py:737
  38.9 0.0 copy-done.2
  38.9 1.7 %fusion.1 = (f32[4,192]{1,0:T(4,128)S(1)}, bf16[4,192,1024]{2,1,0:T(8,128)(2,1)S(1)}) fusion(bf16[4,192,256]{2,1,0:T(8,128)(2,1)} %bitcast.103, bf16[256,1024]{1,0:T(8,128)(2,1)S(1)} %copy-done.2), kind=kOutput, calls=%fused_computation.5 | convolution fusion | flops 405798144 | bytes 2493440 | tf_op jit(solution)/shard_map/btc,cd->btd/dot_general | solution.py:23
  40.6 0.3 fusion.2
  40.9 0.0 copy-done
  40.9 2.4 %fusion.12.proj_ref = bf16[4,192,768]{2,1,0:T(8,128)(2,1)} fusion(bf16[4,192,1024]{2,1,0:T(8,128)(2,1)S(1)} %fusion.2, bf16[1024,768]{1,0:T(8,128)(2,1)S(1)} %copy-done), kind=kOutput, calls=%fused_computation.18 | convolution fusion | flops 1208549376 | bytes 4325376 | tf_op jit(solution)/shard_map/btd,de->bte/dot_general | solution.py:23
  43.3 12.5 %attention.1 = (bf16[4,192,256]{2,1,0:T(8,128)(2,1)}, bf16[4,192,768]{2,1,0:T(8,128)(2,1)}) custom-call(s32[4]{0:T(128)} %slice_reduce_fusion.len_ref, bf16[4,192,768]{2,1,0:T(8,128)(2,1)} %fusion.12.proj_ref, bf16[4,192,256]{2,1,0:T(8,128)(2,1)} %bitcast.91), custom_call_target="tpu_custom_call" | custom-call | tf_op jit(solution)/shard_map/attention/pallas_call | solution.py:157
  55.8 2.8 %fusion.8 = f32[4,192,1024]{2,1,0:T(8,128)S(1)} fusion(bf16[4,192,768]{2,1,0:T(8,128)(2,1)} %get-tuple-element.31, bf16[1024,768]{1,0:T(8,128)(2,1)S(1)} %copy-done), kind=kOutput, calls=%fused_computation.14 | convolution fusion | flops 1207959552 | bytes 5898240 | tf_op jit(solution)/shard_map/bte,de->btd/dot_general | solution.py:23
  58.6 1.5 %fusion.6 = bf16[4,192,1024]{2,1,0:T(8,128)(2,1)S(1)} fusion(bf16[4,192,1024]{2,1,0:T(8,128)(2,1)S(1)} %copy-done.5, f32[4,192,1024]{2,1,0:T(8,128)S(1)} %fusion.8, f32[4,192]{1,0:T(4,128)S(1)} %get-tuple-element.45, f32[4,192]{1,0:T(4,128)S(1)} %get-tuple-element.46), kind=kOutput, calls=%fused_computation.10 | output fusion | flops 7079679 | bytes 6297600 | tf_op jit(solution)/shard_map/mul | solution.py:751
  60.1 0.0 copy-start.12
  60.1 1.1 copy-done.12
  61.3 0.0 copy-done.13
  61.3 1.5 fusion.15
  62.7 1.6 %dynamic-slice_bitcast_fusion.refs_0_ = bf16[4,1,24,1024]{3,2,1,0:T(8,128)(2,1)} fusion(bf16[4,192,1024]{2,1,0:T(8,128)(2,1)} %copy-done.12, s32[]{:T(128)S(6)} %select_n.24), kind=kLoop, calls=%fused_computation.39 | loop fusion | bytes 393220 | tf_op jit(solution)/shard_map/reshape | solution.py:759
  64.4 6.2 %exchange_stream_2.1 = f32[1,24,1024]{2,1,0:T(8,128)} custom-call(bf16[4,1,24,1024]{3,2,1,0:T(8,128)(2,1)} %dynamic-slice_bitcast_fusion.refs_0_), custom_call_target="tpu_custom_call" | custom-call | tf_op jit(solution)/shard_map/exchange_stream_2/pallas_call | solution.py:102
  70.6 0.0 copy-done.10
  70.6 1.1 fusion.21
  71.8 0.6 convert_element_type.75.dr_ref
  72.4 0.1 fusion.25
  72.5 0.6 pad_add_fusion.info_ref
  73.2 0.0 copy-done.1
  73.2 1.7 %fusion.16.refs_0_ = bf16[4,1,24,1024]{3,2,1,0:T(8,128)(2,1)} fusion(bf16[256,1024]{1,0:T(8,128)(2,1)S(1)} %copy-done.1, bf16[4,192,256]{2,1,0:T(8,128)(2,1)} %get-tuple-element.32, s32[]{:T(128)S(6)} %select_n.24), kind=kOutput, calls=%fused_computation.23 | convolution fusion | flops 50429952 | bytes 770052 | tf_op jit(solution)/shard_map/bte,ed->btd/dot_general | solution.py:23
  74.9 0.6 copy.21.dh_ref
  75.5 17.4 %conv_backward.1 = (bf16[6144,256]{1,0:T(8,128)(2,1)}, bf16[512,256]{1,0:T(8,128)(2,1)}, bf16[512,512]{1,0:T(8,128)(2,1)}, f32[1,24,1024]{2,1,0:T(8,128)}, f32[64,1024]{1,0:T(8,128)}) custom-call(s32[2]{0:T(128)} %pad_add_fusion.info_ref, bf16[512,256]{1,0:T(8,128)(2,1)} %get-tuple-element.27.in_ref, bf16[6144,256]{1,0:T(8,128)(2,1)} %bitcast.89, ...), custom_call_target="tpu_custom_call" | custom-call | tf_op jit(solution)/shard_map/conv_backward/pallas_call | solution.py:382
  92.9 0.0 copy-start.6
  92.9 1.4 collective-permute-start
  94.3 2.0 %convolution_bitcast_fusion.3 = bf16[256,128]{1,0:T(8,128)(2,1)} fusion(bf16[4,8,24,256]{3,2,1,0:T(8,128)(2,1)} %get-tuple-element.26, bf16[8,4,24,128]{3,2,1,0:T(8,128)(2,1)} %get-tuple-element.40), kind=kOutput, calls=%fused_computation.26 | convolution fusion | flops 50331648 | bytes 655360 | tf_op jit(solution)/shard_map/btc,btd->cd/dot_general | solution.py:23
  96.3 0.9 copy.22
  97.2 2.0 %convolution_bitcast_fusion.2 = f32[256,128]{1,0:T(8,128)} fusion(bf16[4,192,256]{2,1,0:T(8,128)(2,1)} %get-tuple-element.32, bf16[4,192,128]{2,1,0:T(8,128)(2,1)S(1)} %bitcast.92), kind=kOutput, calls=%fused_computation.25 | convolution fusion | flops 50331648 | bytes 720896 | tf_op jit(solution)/shard_map/bte,btd->ed/dot_general | solution.py:23
  99.2 0.0 copy-done.6
  99.2 2.0 %convolution_bitcast_fusion.1 = f32[128,768]{1,0:T(8,128)} fusion(bf16[4,192,768]{2,1,0:T(8,128)(2,1)S(1)} %copy-done.6, bf16[4,192,1024]{2,1,0:T(8,128)(2,1)} %copy-done.3, s32[]{:T(128)S(6)} %select_n.26), kind=kOutput, calls=%fused_computation.21 | convolution fusion | flops 150994944 | bytes 1769476 | tf_op jit(solution)/shard_map/btd,bte->de/dot_general | solution.py:23
  101.2 1.7 %convolution_convert_fusion.2 = bf16[256,256]{1,0:T(8,128)(2,1)} fusion(f32[24,256]{1,0:T(8,128)} %get-tuple-element.37, bf16[24,256]{1,0:T(8,128)(2,1)S(1)} %fusion.21), kind=kOutput, calls=%fused_computation.24 | convolution fusion | flops 18939904 | bytes 167936 | tf_op jit(solution)/shard_map/dot_general | solution.py:764
  102.9 1.7 %fusion.20 = bf16[1,24,1024]{2,1,0:T(8,128)(2,1)} fusion(f32[1,24,1024]{2,1,0:T(8,128)} %get-tuple-element.33, bf16[256,1024]{1,0:T(8,128)(2,1)S(1)} %copy-done.2, bf16[4,8,24,256]{3,2,1,0:T(8,128)(2,1)} %get-tuple-element.26, s32[]{:T(128)S(6)} %select_n.21, s32[]{:T(128)S(6)} %select_n.23), kind=kOutput, calls=%fused_computation.31 | convolution fusion | flops 12681216 | bytes 684040 | tf_op jit(solution)/shard_map/btc,cd->btd/dot_general | solution.py:23
  104.7 1.3 dynamic-slice_convert_fusion.refs_2_
  106.0 3.6 %slice.10 = bf16[5632,256]{1,0:T(8,128)(2,1)} slice(bf16[6144,256]{1,0:T(8,128)(2,1)} %get-tuple-element.34), slice={[0:5632], [0:256]} | slice | bytes 5767168 | tf_op jit(solution)/shard_map/slice | solution.py:788
  109.6 11.6 %exchange_stream_3.1 = (bf16[128,512]{1,0:T(8,128)(2,1)}, bf16[64,256]{1,0:T(8,128)(2,1)}) custom-call(bf16[4,128,512]{2,1,0:T(8,128)(2,1)} %bitcast.94, bf16[4,64,256]{2,1,0:T(8,128)(2,1)} %bitcast.95), custom_call_target="tpu_custom_call" | custom-call | tf_op jit(solution)/shard_map/exchange_stream_3/pallas_call | solution.py:102
  121.2 19.7 %final_sums.1 = (f32[8,16,512]{2,1,0:T(8,128)}, f32[8,8,256]{2,1,0:T(8,128)}, f32[8,64,128]{2,1,0:T(8,128)}) custom-call(bf16[8,16,512]{2,1,0:T(8,128)(2,1)} %bitcast.100, bf16[8,8,256]{2,1,0:T(8,128)(2,1)} %bitcast.102, bf16[64,128]{1,0:T(8,128)(2,1)} %dynamic-slice_convert_fusion.refs_2_), custom_call_target="tpu_custom_call" | custom-call | tf_op jit(solution)/shard_map/final_sums/pallas_call | solution.py:355
  140.9 1.7 %bitcast_add_fusion = f32[64,1024]{1,0:T(8,128)} fusion(f32[64,1024]{1,0:T(8,128)S(1)} %copy-done.8, f32[8,64,128]{2,1,0:T(8,128)} %get-tuple-element.44), kind=kLoop, calls=%fused_computation.37 | loop fusion | flops 65536 | bytes 786432 | tf_op jit(solution)/shard_map/add | solution.py:806
  142.6 0.0 collective-permute-done
  142.6 1.0 add_convert_fusion
  143.6 3.7 %maximum_bitcast_fusion = bf16[1,6144,256]{2,1,0:T(8,128)(2,1)} fusion(bf16[512,256]{1,0:T(8,128)(2,1)S(1)} %add_convert_fusion, bf16[5632,256]{1,0:T(8,128)(2,1)} %slice.10), kind=kLoop, calls=%fused_computation.11 | loop fusion | flops 6291456 | bytes 6291456 | tf_op jit(solution)/shard_map/broadcast_in_dim | solution.py:788
  147.4 0.7 copy.35
  148.1 0.0 copy-done.11
  148.1 0.6 copy.36
  (18 shorter events, 0.1 us)
Async XLA Ops:
  0.6 40.3 %copy-start = (bf16[1024,768]{1,0:T(8,128)(2,1)S(1)}, bf16[1024,768]{1,0:T(8,128)(2,1)}, u32[]{:S(2)}) copy-start(bf16[1024,768]{1,0:T(8,128)(2,1)} %param.13) | copy-start | bytes 4718596
  0.6 38.2 %copy-start.2 = (bf16[256,1024]{1,0:T(8,128)(2,1)S(1)}, bf16[256,1024]{1,0:T(8,128)(2,1)}, u32[]{:S(2)}) copy-start(bf16[256,1024]{1,0:T(8,128)(2,1)} %param.12) | copy-start | bytes 1572868
  40.5 2.8 %copy-start.4 = (bf16[4,192,1024]{2,1,0:T(8,128)(2,1)}, bf16[4,192,1024]{2,1,0:T(8,128)(2,1)S(1)}, u32[]{:S(2)}) copy-start(bf16[4,192,1024]{2,1,0:T(8,128)(2,1)S(1)} %get-tuple-element.48) | copy-start | bytes 4718596
  40.9 2.4 %copy-start.3 = (bf16[4,192,1024]{2,1,0:T(8,128)(2,1)}, bf16[4,192,1024]{2,1,0:T(8,128)(2,1)S(1)}, u32[]{:S(2)}) copy-start(bf16[4,192,1024]{2,1,0:T(8,128)(2,1)S(1)} %fusion.2) | copy-start | bytes 4718596
  55.8 2.8 %copy-start.5 = (bf16[4,192,1024]{2,1,0:T(8,128)(2,1)S(1)}, bf16[4,192,1024]{2,1,0:T(8,128)(2,1)}, u32[]{:S(2)}) copy-start(bf16[4,192,1024]{2,1,0:T(8,128)(2,1)} %copy-done.4) | copy-start | bytes 4718596
  58.6 2.7 %copy-start.13 = (bf16[4,8,24,256]{3,2,1,0:T(8,128)(2,1)S(1)}, bf16[4,8,24,256]{3,2,1,0:T(8,128)(2,1)}, u32[]{:S(2)}) copy-start(bf16[4,8,24,256]{3,2,1,0:T(8,128)(2,1)} %get-tuple-element.26) | copy-start | bytes 1179652
  60.1 1.1 copy-start.12
  61.3 9.3 %copy-start.10 = (bf16[1,24,1024]{2,1,0:T(8,128)(2,1)S(1)}, bf16[1,24,1024]{2,1,0:T(8,128)(2,1)}, u32[]{:S(2)}) copy-start(bf16[1,24,1024]{2,1,0:T(8,128)(2,1)} %param.15) | copy-start | bytes 147460
  61.3 11.1 %copy-start.7 = (bf16[256,256]{1,0:T(8,128)(2,1)S(1)}, bf16[256,256]{1,0:T(8,128)(2,1)}, u32[]{:S(2)}) copy-start(bf16[256,256]{1,0:T(8,128)(2,1)} %wres_ref.1) | copy-start | bytes 393220
  61.3 11.9 %copy-start.1 = (bf16[256,1024]{1,0:T(8,128)(2,1)S(1)}, bf16[256,1024]{1,0:T(8,128)(2,1)}, u32[]{:S(2)}) copy-start(bf16[256,1024]{1,0:T(8,128)(2,1)} %wout_ref.1) | copy-start | bytes 1572868
  92.9 6.3 %copy-start.6 = (bf16[4,192,768]{2,1,0:T(8,128)(2,1)S(1)}, bf16[4,192,768]{2,1,0:T(8,128)(2,1)}, u32[]{:S(2)}) copy-start(bf16[4,192,768]{2,1,0:T(8,128)(2,1)} %get-tuple-element.31) | copy-start | bytes 3538948
  92.9 49.7 %collective-permute-start = (bf16[512,256]{1,0:T(8,128)(2,1)}, bf16[512,256]{1,0:T(8,128)(2,1)S(1)}, u32[]{:S(2)}, u32[]{:S(2)}) collective-permute-start(bf16[512,256]{1,0:T(8,128)(2,1)} %get-tuple-element.35), channel_id=1, source_target_pairs={{4,0},{8,4},{12,8},{16,12},{20,16},{24,20},{28,24},{5,1},{9,5},{13... | collective-permute-start | bytes 786440 | tf_op jit(solution)/shard_map/ppermute | solution.py:713
  106.0 34.9 %copy-start.8 = (f32[64,1024]{1,0:T(8,128)S(1)}, f32[64,1024]{1,0:T(8,128)}, u32[]{:S(2)}) copy-start(f32[64,1024]{1,0:T(8,128)} %get-tuple-element.43) | copy-start | bytes 786436
  143.6 3.7 %copy-start.9 = (f32[8,16,512]{2,1,0:T(8,128)S(1)}, f32[8,16,512]{2,1,0:T(8,128)}, u32[]{:S(2)}) copy-start(f32[8,16,512]{2,1,0:T(8,128)} %get-tuple-element.41) | copy-start | bytes 786436
  143.6 4.4 %copy-start.11 = (f32[8,8,256]{2,1,0:T(8,128)S(1)}, f32[8,8,256]{2,1,0:T(8,128)}, u32[]{:S(2)}) copy-start(f32[8,8,256]{2,1,0:T(8,128)} %get-tuple-element.42) | copy-start | bytes 196612

commit v2 on v1

v2 whole, which is shorter than its diff:
```python
import functools
import math

import jax
import jax.numpy as jnp
from jax import lax
from jax.experimental import pallas as pl
from jax.experimental.pallas import tpu as pltpu
from jax.sharding import PartitionSpec as P

HEADS = 16
POOL = 256
DILATION_STEP = 512
EPS = 1e-05
BF16 = jnp.bfloat16
F32 = jnp.float32
MESH = pl.DeviceIdType.MESH
VMEM_SPEC = pl.BlockSpec(memory_space=pltpu.VMEM)


def device_of(tm, stream):
    return {"tm": tm, "stream": stream}


def front_kernel(
    steps, group, len_ref, sig_hbm, w_ref, wout_ref, wres_ref, wgrad_ref,
    a_hbm, edge_hbm, hsum_ref, pool_ref, ctx_ref, cols_ref, lens_ref,
    sig, a_buf, grads, gate_w, ctx_mine, cols_mine, sums, sem_in, sem_out, send_tm, recv_tm,
    send_st, recv_st, send_pool, recv_pool, send_near, recv_near, keep,
):
    tms, parts = lax.axis_size("tm"), lax.axis_size("stream")
    tm, st = lax.axis_index("tm"), lax.axis_index("stream")
    chips = parts // 2
    core, chip = lax.rem(st, 2), st // 2
    mine = tm * chips + chip
    tile = DILATION_STEP
    samples = steps * tile
    chans = w_ref.shape[1] // 2
    toks = samples // POOL
    rounds = steps // group

    def peer_of(flat):
        return device_of(flat // chips, lax.rem(flat, chips) * 2 + core)

    barrier = pltpu.get_barrier_semaphore()

    def greet(device):
        pl.semaphore_signal(barrier, inc=1, device_id=device, device_id_type=MESH)

    others = tms * chips
    lax.fori_loop(1, others, lambda d, c: (greet(peer_of(lax.rem(mine + d, others))), c)[1], 0)
    for d in range(chips):
        greet(device_of(tm, lax.rem(chip + d, chips) * 2 + 1 - core))

    def load(i):
        return pltpu.make_async_copy(
            sig_hbm.at[pl.ds(i * tile, tile)], sig.at[pl.ds((i + 1) * tile, tile)], sem_in.at[i]
        )

    def save(i):
        return pltpu.make_async_copy(
            a_buf.at[pl.ds(i * tile, tile)], a_hbm.at[pl.ds(i * tile, tile)], sem_out.at[i]
        )

    for i in reversed(range(steps)):
        load(i).start()
    gate_w[...] = w_ref[:, chans:] * jnp.asarray(0.5, BF16)

    halo = pltpu.make_async_remote_copy(
        src_ref=sig_hbm.at[pl.ds(samples - tile, tile)],
        dst_ref=sig.at[pl.ds(0, tile)],
        send_sem=send_tm.at[2, 0],
        recv_sem=recv_tm.at[2, 0],
        device_id={"tm": lax.rem(tm + 1, tms)},
        device_id_type=MESH,
    )

    def to_stream(j, d, src, dst):
        return pltpu.make_async_remote_copy(
            src_ref=src,
            dst_ref=dst,
            send_sem=send_st.at[j, d - 1],
            recv_sem=recv_st.at[j, d - 1],
            device_id={"stream": lax.rem(st + d, parts)},
            device_id_type=MESH,
        )

    grad_copies = [
        copy
        for d in range(1, parts)
        for copy in (
            to_stream(0, d, wgrad_ref, grads.at[st]),
            to_stream(1, d, lens_ref.at[st], lens_ref.at[st]),
        )
    ]

    def to_tm(j, d, src, dst):
        return pltpu.make_async_remote_copy(
            src_ref=src,
            dst_ref=dst,
            send_sem=send_tm.at[j, d - 1],
            recv_sem=recv_tm.at[j, d - 1],
            device_id={"tm": lax.rem(tm + d, tms)},
            device_id_type=MESH,
        )

    width = grads.shape[2]
    columns = width // tms

    tm_copies = [
        copy
        for d in range(1, tms)
        for copy in (
            to_tm(0, d, ctx_mine, ctx_ref.at[tm]),
            to_tm(1, d, cols_mine.at[lax.rem(tm + d, tms)], cols_ref.at[tm]),
        )
    ]
    own_grad = pltpu.make_async_copy(wgrad_ref, grads.at[st], keep.at[0])
    own_ctx = pltpu.make_async_copy(ctx_mine, ctx_ref.at[tm], keep.at[1])
    own_cols = pltpu.make_async_copy(cols_mine.at[tm], cols_ref.at[tm], keep.at[2])
    edge = pltpu.make_async_copy(sig.at[pl.ds(0, tile)], edge_hbm, keep.at[3])

    lens_ref[st] = jnp.full(lens_ref.shape[1:], len_ref[0], jnp.int32)
    length = len_ref[0]

    def chunk(token):
        base = token * POOL
        past = sig[pl.ds(base, POOL), :]
        cur = sig[pl.ds(base + tile, POOL), :]
        mixed_f = jnp.dot(past, w_ref[:chans, :chans], preferred_element_type=F32)
        mixed_f += jnp.dot(cur, w_ref[chans:, :chans], preferred_element_type=F32)
        mixed_g = jnp.dot(past, gate_w[:chans], preferred_element_type=F32)
        mixed_g += jnp.dot(cur, gate_w[chans:], preferred_element_type=F32)
        row = lax.broadcasted_iota(jnp.int32, (POOL, 128), 0) + (tm * samples + base)
        half = jnp.where(row < length, 0.5, 0.0)
        half = jnp.concatenate([half] * (chans // 128), axis=1)
        t = jnp.tanh(mixed_f)
        s = half * jnp.tanh(mixed_g) + half
        h = t * s
        a_buf[pl.ds(base, POOL), :chans] = (s - t * h).astype(BF16)
        a_buf[pl.ds(base, POOL), chans:] = (h - h * s).astype(BF16)
        hs = jnp.sum(h, axis=0, keepdims=True)
        ss = jnp.sum(cur.astype(F32) * half, axis=0, keepdims=True) * 2.0
        return hs, ss

    def body(it, carry):
        r = rounds - 1 - it
        per_tile = tile // POOL
        rows = [None] * (group * per_tile)
        for k in reversed(range(group)):
            i = r * group + k
            if k > 0:
                load(i - 1).wait()
            else:

                @pl.when(r > 0)
                def _():
                    load(i - 1).wait()

                @pl.when((r == 0) & (tm > 0))
                def _():
                    halo.wait_recv()

                @pl.when((r == 0) & (tm == 0))
                def _():
                    sig[pl.ds(0, tile), :] = jnp.zeros((tile, chans), BF16)

            for j in range(per_tile):
                rows[k * per_tile + j] = chunk(i * per_tile + j)
            save(i).start()
        block = pl.ds(pl.multiple_of(r * group * per_tile, 8), group * per_tile)
        hsum_ref[block, :] = jnp.concatenate([a for a, _ in rows], axis=0)
        sums[block, :] = jnp.concatenate([b for _, b in rows], axis=0)

        @pl.when(it == 0)
        def _():
            pl.semaphore_wait(barrier, others - 1 + chips)

            @pl.when(tm < tms - 1)
            def _():
                halo.start()
            own_grad.start()
            for copy in grad_copies:
                copy.start()

        @pl.when(it == 1)
        def _():
            own_grad.wait()
            for copy in grad_copies:
                copy.wait()
            for p in range(parts):
                ctx_mine[p] = lax.dot_general(
                    grads[p], wout_ref[...], (((1,), (1,)), ((), ())), preferred_element_type=F32
                ).astype(BF16)
                for k in range(tms):
                    cols_mine[k, p] = grads[p, :, k * columns : (k + 1) * columns]
            own_ctx.start()
            own_cols.start()
            for copy in tm_copies:
                copy.start()

        return carry

    load(steps - 1).wait()
    lax.fori_loop(0, rounds, body, 0)
    edge.start()

    total = hsum_ref[...]
    high = total.astype(BF16)
    low = (total - high.astype(F32)).astype(BF16)
    resid = jnp.dot(high, wres_ref[...], preferred_element_type=F32)
    resid += jnp.dot(low, wres_ref[...], preferred_element_type=F32)
    pool_ref[st, tm] = ((sums[...] + resid) / POOL).astype(BF16)

    def spread(d):
        return pltpu.make_async_remote_copy(
            src_ref=pool_ref.at[st, tm],
            dst_ref=pool_ref.at[st, tm],
            send_sem=send_pool.at[d],
            recv_sem=recv_pool.at[d],
            device_id=peer_of(lax.rem(mine + d, others)),
            device_id_type=MESH,
        )

    def relay(d):
        flat = lax.rem(mine - d + others, others)
        block = pool_ref.at[lax.rem(flat, chips) * 2 + core, flat // chips]
        return pltpu.make_async_remote_copy(
            src_ref=block,
            dst_ref=block,
            send_sem=send_near.at[d],
            recv_sem=recv_near.at[d],
            device_id={"stream": chip * 2 + 1 - core},
            device_id_type=MESH,
        )

    def launch(d, c):
        spread(d).start()
        return c

    def forward(d, c):
        spread(d).wait_recv()
        relay(d).start()
        return c

    def settle(d, c):
        spread(d).wait_send()
        return c

    def close(d, c):
        relay(d).wait()
        return c

    lax.fori_loop(1, others, launch, 0)
    relay(0).start()
    lax.fori_loop(1, others, forward, 0)
    for copy in tm_copies:
        copy.wait()
    own_ctx.wait()
    own_cols.wait()
    edge.wait()
    for i in range(steps):
        save(i).wait()

    @pl.when(tm < tms - 1)
    def _():
        halo.wait_send()

    lax.fori_loop(1, others, settle, 0)
    lax.fori_loop(0, others, close, 0)


def front(lengths, signal, w_conv, w_out, w_res, d_out, collective):
    samples, chans = signal.shape
    toks, width = d_out.shape
    tms, parts = lax.axis_size("tm"), lax.axis_size("stream")
    steps = samples // DILATION_STEP
    group = 4
    inner = w_out.shape[0]
    others = tms * parts // 2
    columns = width // tms
    anywhere = pl.BlockSpec(memory_space=pl.ANY)
    dma = pltpu.SemaphoreType.DMA
    return pl.pallas_call(
        functools.partial(front_kernel, steps, group),
        out_shape=[
            jax.ShapeDtypeStruct((samples, 2 * chans), BF16),
            jax.ShapeDtypeStruct((DILATION_STEP, chans), BF16),
            jax.ShapeDtypeStruct((toks, chans), F32),
            jax.ShapeDtypeStruct((parts, tms, toks, chans), BF16),
            jax.ShapeDtypeStruct((tms, parts, toks, inner), BF16),
            jax.ShapeDtypeStruct((tms, parts, toks, columns), BF16),
            jax.ShapeDtypeStruct((parts, 8, 128), jnp.int32),
        ],
        in_specs=[pl.BlockSpec(memory_space=pltpu.SMEM), anywhere] + [VMEM_SPEC] * 4,
        out_specs=[anywhere, anywhere] + [VMEM_SPEC] * 5,
        scratch_shapes=[
            pltpu.VMEM((samples + DILATION_STEP, chans), BF16),
            pltpu.VMEM((samples, 2 * chans), BF16),
            pltpu.VMEM((parts, toks, width), BF16),
            pltpu.VMEM((2 * chans, chans), BF16),
            pltpu.VMEM((parts, toks, inner), BF16),
            pltpu.VMEM((tms, parts, toks, columns), BF16),
            pltpu.VMEM((toks, chans), F32),
            dma((steps,)),
            dma((steps,)),
            dma((3, tms - 1)),
            dma((3, tms - 1)),
            dma((2, parts - 1)),
            dma((2, parts - 1)),
            dma((others,)),
            dma((others,)),
            dma((others,)),
            dma((others,)),
            dma((4,)),
        ],
        compiler_params=pltpu.CompilerParams(collective_id=collective, has_side_effects=True),
        name="front",
    )(lengths, signal, w_conv, w_out, w_res, d_out)


NT = (((1,), (1,)), ((), ()))
TN = (((0,), (0,)), ((), ()))


def fdot(a, b, dims=(((1,), (0,)), ((), ()))):
    return lax.dot_general(a, b, dims, preferred_element_type=F32)


def attend(heads, size, allowed, proj, dctx, ctx, dproj):
    scale = 1.0 / math.sqrt(size)
    span = range(heads)

    def part(h, j):
        base = (3 * h + j) * size
        return proj[:, base : base + size]

    inner = [slice(h * size, (h + 1) * size) for h in span]
    scores = [fdot(part(h, 0), part(h, 1), NT) * scale for h in span]
    d_prob = [fdot(dctx[:, inner[h]], part(h, 2), NT) for h in span]
    scores = [jnp.where(allowed, a, -1e30) for a in scores]
    weights = [jnp.exp(a - jnp.max(a, axis=-1, keepdims=True)) for a in scores]
    prob = [a * (1.0 / jnp.sum(a, axis=-1, keepdims=True)) for a in weights]
    prob16 = [a.astype(BF16) for a in prob]
    d_score = [
        (p * (d - jnp.sum(d * p, axis=-1, keepdims=True))).astype(BF16)
        for p, d in zip(prob, d_prob)
    ]
    for h in span:
        base = 3 * h * size
        ctx[:, inner[h]] = fdot(prob16[h], part(h, 2))
        d_query = scale * fdot(d_score[h], part(h, 1))
        d_key = scale * fdot(d_score[h], part(h, 0), TN)
        d_value = fdot(prob16[h], dctx[:, inner[h]], TN)
        dproj[:, base : base + size] = d_query.astype(BF16)
        dproj[:, base + size : base + 2 * size] = d_key.astype(BF16)
        dproj[:, base + 2 * size : base + 3 * size] = d_value.astype(BF16)


def back_kernel(
    steps, heads, len_ref, lens_ref, sig_hbm, edge_hbm, a_hbm, hsum_ref, pool_ref, ctx_in, cols_in,
    w_ref, wres_ref, win_ref, wqkv_ref, wout_ref, grad_ref,
    out_ref, dsig_hbm, gconv_ref, gres_ref, gin_ref, gqkv_ref, gout_ref,
    sig, a_buf, dsig, first, arrive, pool_f, pool_b, dctx_f, dctx_b, cols_f, cols_b, tok_v, norm,
    proj, ctx_v, dproj, dg, gin_acc, cols_acc, own_send, own_land, out_send, out_land, cols_mine,
    cols_land, in_parts, in_near, in_sum, in_far, conv_acc, conv_parts, conv_near, conv_sum,
    conv_far, conv_f, conv_rows, conv_rland, conv_own, conv_land, res_acc, res_parts, res_near,
    res_sum, res_far, res_f, res_rows, res_rland, res_own, res_land, dh8, dr8,
    sem_in, sem_a, sem_out, send, recv,
):
    tms, parts = lax.axis_size("tm"), lax.axis_size("stream")
    tm, st = lax.axis_index("tm"), lax.axis_index("stream")
    chips = parts // 2
    core, chip = lax.rem(st, 2), st // 2
    tile = DILATION_STEP
    samples = steps * tile
    chans = w_ref.shape[1] // 2
    toks, width = grad_ref.shape
    total = tms * toks
    inner = wout_ref.shape[0]
    size = inner // heads
    columns = width // tms
    in_rows = chans // parts

    barrier = pltpu.get_barrier_semaphore()
    for d in range(1, parts):
        pl.semaphore_signal(
            barrier, inc=1, device_id={"stream": lax.rem(st + d, parts)}, device_id_type=MESH
        )
    for d in range(1, tms):
        pl.semaphore_signal(
            barrier, inc=1, device_id={"tm": lax.rem(tm + d, tms)}, device_id_type=MESH
        )

    loads = [pltpu.make_async_copy(edge_hbm, sig.at[pl.ds(0, tile)], sem_in.at[0])]
    loads.append(pltpu.make_async_copy(sig_hbm, sig.at[pl.ds(tile, samples)], sem_in.at[1]))
    loads.append(pltpu.make_async_copy(a_hbm, a_buf, sem_a.at[0]))
    for copy in loads:
        copy.start()

    count = iter(range(send.shape[0]))

    def remote(src, dst, device):
        j = next(count)
        return pltpu.make_async_remote_copy(
            src_ref=src,
            dst_ref=dst,
            send_sem=send.at[j],
            recv_sem=recv.at[j],
            device_id=device,
            device_id_type=MESH,
        )

    def to_stream(d):
        return {"stream": lax.rem(st + d, parts)}

    def to_tm(d):
        return {"tm": lax.rem(tm + d, tms)}

    def to_chip(d):
        return {"stream": lax.rem(chip + d, chips) * 2 + core}

    near = {"stream": chip * 2 + 1 - core}

    def begin(copies):
        for copy in copies:
            copy.start()

    def finish(copies):
        for copy in copies:
            copy.wait()

    row = lax.broadcasted_iota(jnp.int32, (total, total), 0)
    col = lax.broadcasted_iota(jnp.int32, (total, total), 1)
    gout_ref[...] = jnp.zeros_like(gout_ref)
    gqkv_ref[...] = jnp.zeros_like(gqkv_ref)
    gin_acc[...] = jnp.zeros_like(gin_acc)
    cols_acc[...] = jnp.zeros_like(cols_acc)
    mine = pl.ds(pl.multiple_of(tm * toks, 8), toks)

    def stay(s, carry):
        for k in range(tms):
            rows = slice(k * toks, (k + 1) * toks)
            pool_f[rows, :] = pool_ref[s, k].astype(F32)
            dctx_f[rows, :] = ctx_in[k, s].astype(F32)
            cols_f[rows, :] = cols_in[k, s].astype(F32)
        pool_b[...] = pool_f[...].astype(BF16)
        dctx_b[...] = dctx_f[...].astype(BF16)
        cols_b[...] = cols_f[...].astype(BF16)
        tok = fdot(pool_b[...], win_ref[...]).astype(BF16).astype(F32)
        tok_v[...] = tok
        r = lax.rsqrt(jnp.mean(tok * tok, axis=-1, keepdims=True) + EPS)
        norm[...] = (tok * r).astype(BF16)
        proj[...] = fdot(norm[...], wqkv_ref[...]).astype(BF16)
        limit = lens_ref[s, 0:1, 0:1]
        allowed = (col <= row) & (col * POOL < limit)
        attend(heads, size, allowed, proj, dctx_b, ctx_v, dproj)
        context = ctx_v[...].astype(BF16)
        gout_ref[...] += fdot(context, cols_b[...], TN)
        cols_acc[...] += fdot(pool_b[...], cols_b[...], TN)
        if columns % 128 == 0:
            own = norm[:, pl.ds(pl.multiple_of(tm * columns, columns), columns)]
            gqkv_ref[...] += fdot(own, dproj[...], TN)
        else:
            for k in range(tms):

                @pl.when(tm == k)
                def _():
                    own = norm[:, k * columns : (k + 1) * columns]
                    gqkv_ref[...] += fdot(own, dproj[...], TN)

        d_normed = fdot(dproj[...], wqkv_ref[...], NT)
        tok = tok_v[...]
        along = jnp.sum(d_normed * tok, axis=-1, keepdims=True)
        d_group = r * d_normed - tok * (r * r * r * along / width)
        dg[...] = d_group
        own_send[s] = dg[mine, :].astype(BF16)
        out_send[s] = fdot(ctx_v[mine, :].astype(BF16), wout_ref[...]).astype(BF16)
        gin_acc[...] += fdot(pool_b[...], d_group.astype(BF16), TN)
        return carry

    lax.fori_loop(0, parts, stay, 0)

    own_copies = [
        remote(own_send.at[lax.rem(st + d, parts)], own_land.at[d - 1], to_stream(d))
        for d in range(1, parts)
    ]
    out_copies = [
        remote(out_send.at[lax.rem(st + d, parts)], out_land.at[d - 1], to_stream(d))
        for d in range(1, parts)
    ]
    cols_copies = [remote(cols_mine, cols_land.at[tm], to_tm(d)) for d in range(1, tms)]
    back = remote(first, arrive, {"tm": lax.rem(tm + tms - 1, tms)})

    def reduce_near(blocks, land):
        return [remote(blocks.at[1 - core], land, near)]

    def reduce_far(sums, land):
        return [
            remote(sums.at[lax.rem(chip + d, chips)], land.at[d - 1], to_chip(d))
            for d in range(1, chips)
        ]

    in_one = reduce_near(in_parts, in_near)
    in_two = reduce_far(in_sum, in_far)
    conv_one = reduce_near(conv_parts, conv_near) + reduce_near(res_parts, res_near)
    conv_two = reduce_far(conv_sum, conv_far) + reduce_far(res_sum, res_far)
    conv_three = [
        copy
        for d in range(1, tms)
        for copy in (
            remote(conv_rows.at[lax.rem(tm + d, tms)], conv_rland.at[d - 1], to_tm(d)),
            remote(res_rows.at[lax.rem(tm + d, tms)], res_rland.at[d - 1], to_tm(d)),
        )
    ]
    conv_four = [
        copy
        for d in range(1, tms)
        for copy in (
            remote(conv_own, conv_land.at[tm], to_tm(d)),
            remote(res_own, res_land.at[tm], to_tm(d)),
        )
    ]

    def split(acc, blocks):
        rows = blocks.shape[2]
        for c in range(2):
            for q in range(chips):
                base = (q * 2 + c) * rows
                blocks[c, q] = acc[base : base + rows, :].astype(BF16)

    def add_near(blocks, land, sums):
        for q in range(chips):
            sums[q] = (blocks[core, q].astype(F32) + land[q].astype(F32)).astype(BF16)

    def add_far(sums, land):
        value = sums[chip].astype(F32)
        for d in range(1, chips):
            value += land[d - 1].astype(F32)
        return value

    def cut(value, full, rows):
        full[...] = value
        n = rows.shape[1]
        for k in range(tms):
            rows[k] = full[k * n : (k + 1) * n, :].astype(BF16)

    def add_rows(rows, land, own, gathered):
        value = rows[tm].astype(F32)
        for d in range(1, tms):
            value += land[d - 1].astype(F32)
        own[...] = value.astype(BF16)
        gathered[tm] = value.astype(BF16)

    pl.semaphore_wait(barrier, parts - 1 + tms - 1)
    begin(own_copies)
    split(gin_acc, in_parts)
    cols_mine[...] = cols_acc[pl.ds(pl.multiple_of(st * in_rows, 8), in_rows), :].astype(BF16)
    cols_land[tm] = cols_mine[...]
    begin(in_one)
    begin(out_copies)
    begin(cols_copies)
    own_tok = fdot(pool_ref[st, tm], win_ref[...]).astype(BF16).astype(F32)

    finish(own_copies)
    d_tok = own_send[st].astype(F32) + grad_ref[...].astype(F32)
    for d in range(1, parts):
        d_tok += own_land[d - 1].astype(F32)
    d_pooled = fdot(d_tok.astype(BF16), win_ref[...], NT)
    d_res = (d_pooled / POOL).astype(BF16)
    d_hidden = fdot(d_res, wres_ref[...], NT)
    d_resf = d_res.astype(F32)
    for t in range(toks):
        dh8[t] = jnp.broadcast_to(d_hidden[t : t + 1, :], (8, chans))
        dr8[t] = jnp.broadcast_to(d_resf[t : t + 1, :], (8, chans))
    high = hsum_ref[...].astype(BF16)
    low = (hsum_ref[...] - high.astype(F32)).astype(BF16)
    res_acc[...] = fdot(high, d_res, TN) + fdot(low, d_res, TN)
    split(res_acc, res_parts)

    finish(in_one)
    add_near(in_parts, in_near, in_sum)
    begin(in_two)
    finish(loads)

    per_tile = tile // POOL

    def later_of(i):
        return fdot(a_buf[pl.ds(i * tile, tile), :], w_ref[:chans, :], NT).astype(BF16)

    conv_acc[...] = jnp.zeros_like(conv_acc)

    def weigh(i, carry):
        rows = pl.ds(i * tile, tile)
        for j in range(per_tile):
            token = i * per_tile + j
            base = pl.ds(token * POOL, POOL)
            gate = dh8[token]
            for c in range(2):
                lanes = slice(c * chans, (c + 1) * chans)
                a = a_buf[base, lanes].astype(F32).reshape(POOL // 8, 8, chans)
                a_buf[base, lanes] = (a * gate[None]).reshape(POOL, chans).astype(BF16)
        dm = a_buf[rows, :]
        conv_acc[:chans, :] += fdot(sig[rows, :], dm, TN)
        conv_acc[chans:, :] += fdot(sig[pl.ds((i + 1) * tile, tile), :], dm, TN)

        @pl.when(i == 0)
        def _():
            first[...] = later_of(0)

            @pl.when(tm > 0)
            def _():
                back.start()

        return carry

    lax.fori_loop(0, steps, weigh, 0)

    split(conv_acc, conv_parts)
    begin(conv_one)

    length = len_ref[0]

    def emit(i, later):
        rows = pl.ds(i * tile, tile)
        here = fdot(a_buf[rows, :], w_ref[chans:, :], NT)
        for j in range(per_tile):
            token = i * per_tile + j
            index = lax.broadcasted_iota(jnp.int32, (POOL, 128), 0) + (tm * samples + token * POOL)
            valid = jnp.where(index < length, 1.0, 0.0)
            valid = jnp.concatenate([valid] * (chans // 128), axis=1)
            own = dr8[token][None] * valid.reshape(POOL // 8, 8, chans)
            part = slice(j * POOL, (j + 1) * POOL)
            value = own.reshape(POOL, chans) + here[part] + later[part].astype(F32)
            dsig[pl.ds(token * POOL, POOL), :] = value.astype(BF16)
        pltpu.make_async_copy(dsig.at[rows], dsig_hbm.at[rows], sem_out.at[i]).start()

    def emit_step(i, carry):
        emit(i, later_of(i + 1))
        return carry

    cuts = [0, steps // 6, steps // 2, steps - 1]
    lax.fori_loop(cuts[0], cuts[1], emit_step, 0)
    finish(conv_one)
    add_near(conv_parts, conv_near, conv_sum)
    add_near(res_parts, res_near, res_sum)
    begin(conv_two)
    lax.fori_loop(cuts[1], cuts[2], emit_step, 0)
    finish(in_two)
    finish(conv_two)
    cut(add_far(conv_sum, conv_far), conv_f, conv_rows)
    cut(add_far(res_sum, res_far), res_f, res_rows)
    begin(conv_three)
    lax.fori_loop(cuts[2], cuts[3], emit_step, 0)

    @pl.when(tm < tms - 1)
    def _():
        back.wait_recv()

    @pl.when(tm == tms - 1)
    def _():
        arrive[...] = jnp.zeros_like(arrive)

    emit(steps - 1, arrive[...])
    finish(out_copies)
    value = own_tok + out_send[st].astype(F32)
    for d in range(1, parts):
        value += out_land[d - 1].astype(F32)
    out_ref[...] = value.astype(BF16)
    finish(cols_copies)
    total_in = add_far(in_sum, in_far)
    for k in range(tms):
        lanes = slice(k * columns, (k + 1) * columns)
        gin_ref[:, lanes] = total_in[:, lanes] + cols_land[k].astype(F32)

    finish(conv_three)
    add_rows(conv_rows, conv_rland, conv_own, conv_land)
    add_rows(res_rows, res_rland, res_own, res_land)
    begin(conv_four)

    @pl.when(tm > 0)
    def _():
        back.wait_send()

    for i in range(steps):
        rows = pl.ds(i * tile, tile)
        pltpu.make_async_copy(dsig.at[rows], dsig_hbm.at[rows], sem_out.at[i]).wait()
    finish(conv_four)
    for k in range(tms):
        n = conv_land.shape[1]
        gconv_ref[k * n : (k + 1) * n, :] = conv_land[k].astype(F32)
        n = res_land.shape[1]
        gres_ref[k * n : (k + 1) * n, :] = res_land[k].astype(F32)


def back(lengths, lens, signal, edge, gates, hsum, pool, ctx, cols, weights, d_out, heads, collective):
    w_conv, w_res, w_in, w_qkv, w_out = weights
    samples, chans = signal.shape
    toks, width = d_out.shape
    tms, parts = lax.axis_size("tm"), lax.axis_size("stream")
    chips = parts // 2
    steps = samples // DILATION_STEP
    total = toks * tms
    inner = w_out.shape[0]
    triple = w_qkv.shape[1]
    columns = width // tms
    joined = 2 * chans
    conv_n, res_n = joined // parts, chans // parts
    anywhere = pl.BlockSpec(memory_space=pl.ANY)
    dma = pltpu.SemaphoreType.DMA

    def vm(*shape, dtype=BF16):
        return pltpu.VMEM(shape, dtype)

    def reduction(rows, n, lanes):
        return [
            vm(rows, lanes, dtype=F32),
            vm(2, chips, n, lanes),
            vm(chips, n, lanes),
            vm(chips, n, lanes),
            vm(max(chips - 1, 1), n, lanes),
            vm(n, lanes, dtype=F32),
            vm(tms, n // tms, lanes),
            vm(tms - 1, n // tms, lanes),
            vm(n // tms, lanes),
            vm(tms, n // tms, lanes),
        ]

    copies = 2 * (parts - 1) + 5 * (tms - 1) + 1 + 3 + 3 * (chips - 1)
    return pl.pallas_call(
        functools.partial(back_kernel, steps, heads),
        out_shape=[
            jax.ShapeDtypeStruct((toks, width), BF16),
            jax.ShapeDtypeStruct((samples, chans), BF16),
            jax.ShapeDtypeStruct((conv_n, joined), F32),
            jax.ShapeDtypeStruct((res_n, chans), F32),
            jax.ShapeDtypeStruct((res_n, width), F32),
            jax.ShapeDtypeStruct((columns, triple), F32),
            jax.ShapeDtypeStruct((inner, columns), F32),
        ],
        in_specs=[pl.BlockSpec(memory_space=pltpu.SMEM), VMEM_SPEC, anywhere, anywhere, anywhere]
        + [VMEM_SPEC] * 10,
        out_specs=[VMEM_SPEC, anywhere] + [VMEM_SPEC] * 5,
        scratch_shapes=[
            vm(samples + DILATION_STEP, chans),
            vm(samples, joined),
            vm(samples, chans),
            vm(DILATION_STEP, chans),
            vm(DILATION_STEP, chans),
            vm(total, chans, dtype=F32),
            vm(total, chans),
            vm(total, inner, dtype=F32),
            vm(total, inner),
            vm(total, columns, dtype=F32),
            vm(total, columns),
            vm(total, width, dtype=F32),
            vm(total, width),
            vm(total, triple),
            vm(total, inner, dtype=F32),
            vm(total, triple),
            vm(total, width, dtype=F32),
            vm(chans, width, dtype=F32),
            vm(chans, columns, dtype=F32),
            vm(parts, toks, width),
            vm(parts - 1, toks, width),
            vm(parts, toks, width),
            vm(parts - 1, toks, width),
            vm(res_n, columns),
            vm(tms, res_n, columns),
            vm(2, chips, res_n, width),
            vm(chips, res_n, width),
            vm(chips, res_n, width),
            vm(max(chips - 1, 1), res_n, width),
        ]
        + reduction(joined, conv_n, joined)
        + reduction(chans, res_n, chans)
        + [
            vm(toks, 8, chans, dtype=F32),
            vm(toks, 8, chans, dtype=F32),
            dma((2,)),
            dma((1,)),
            dma((steps,)),
            dma((copies,)),
            dma((copies,)),
        ],
        compiler_params=pltpu.CompilerParams(
            collective_id=collective, has_side_effects=True, vmem_limit_bytes=60 * 1024 * 1024
        ),
        name="back",
    )(lengths, lens, signal, edge, gates, hsum, pool, ctx, cols, w_conv, w_res, w_in, w_qkv, w_out, d_out)


def local(signal, lengths, w_conv, w_res, w_in, w_qkv, w_out, d_out):
    samples, chans = signal.shape[1:]
    toks, width = d_out.shape[1:]
    flat, grad = signal.reshape(samples, chans), d_out.reshape(toks, width)
    heads = w_out.shape[0] // (width // HEADS)
    gates, edge, hsum, pool, ctx, cols, lens = front(
        lengths, flat, w_conv, w_out, w_res, grad, 0
    )
    weights = (w_conv, w_res, w_in, w_qkv, w_out)
    out, d_sig, *grads = back(
        lengths, lens, flat, edge, gates, hsum, pool, ctx, cols, weights, grad, heads, 1
    )
    return (out[None], d_sig[None], *grads)


def solution(mesh):
    in_specs = (
        P("stream", "tm", None),
        P("stream"),
        P(),
        P(),
        P(),
        P(None, "stream"),
        P("stream", None),
        P("stream", "tm", None),
    )
    out_specs = (
        P("stream", "tm", None),
        P("stream", "tm", None),
        P("stream", None),
        P("stream", None),
        P("stream", None),
        P("tm", "stream"),
        P("stream", "tm"),
    )
    return jax.shard_map(local, mesh=mesh, in_specs=in_specs, out_specs=out_specs, check_vma=False)
```

time: 150 us -> 96.1 us (0.64)
  matrix products: 20.7 us -> 0 us
  Pallas kernels: 102 us -> 85.8 us
  other arithmetic: 9.49 us -> 0 us
  local copies, waits for them, and re-layouts: 13.9 us -> 8.72 us
    dot_general x12 -> x0, matrix products: 20.7 us -> none  [the longest x10 18.9 us: dot(): return jnp.einsum(eq, a, b, preferred_element_type=F32)]
    pallas_call x5 -> x1, Pallas kernels: 67.3 us -> 51.6 us  [back(): pl.pallas_call(functools.partial(back_kernel, steps, heads), out_shape=[j...]
    unnamed x30 -> x17, local copies, waits for them, and re-layouts: 2.53 us -> 8.72 us
    slice x2 -> x0, local copies, waits for them, and re-layouts: 5.04 us -> none  [the longest x1 3.64 us: local(): d_signal = jnp.concatenate([d_sig[:edge], last], axis=0)[None]]
    broadcast_in_dim x1 -> x0, other arithmetic: 3.73 us -> none  [local(): d_signal = jnp.concatenate([d_sig[:edge], last], axis=0)[None]]
    transpose x2 -> x0, local copies, waits for them, and re-layouts: 2.71 us -> none  [the longest x1 1.77 us: local(): all_ctx = all_ctx.transpose(1, 0, 2, 3).reshape(group, total, heads * size)]
    convert_element_type x3 -> x0, other arithmetic: 1.96 us -> none  [the longest x1 1.01 us: local(): last = (d_sig[edge:].astype(F32) + arriving.astype(F32)).astype(BF16)]
    add x1 -> x0, other arithmetic: 1.68 us -> none  [local(): sum_in = s_in + a_in.transpose(1, 0, 2).reshape(in_rows, width).astype(F32)]
  transfers between devices with their start and end apart: 1 -> 0, of which waited for: 0 -> 0; matrix products, arithmetic and copies ran while one was open for 11% -> 0% of each run, Pallas kernels for 21% -> 0%
where the time goes in v2:
time: 96.1 us; the launch traced here: 95.9 us
  Pallas kernels  85.8 us (89%)
  local copies, waits for them, and re-layouts  8.72 us (9%)
  between operations  1.31 us (1%)
    pallas_call x1, Pallas kernels, back(): pl.pallas_call(functools.partial(back_kernel, steps, heads), out_shape=[j...  51.6 us
    pallas_call x1, Pallas kernels, front(): pl.pallas_call(functools.partial(front_kernel, steps, group), out_shape=[...  34.2 us
    unnamed x17, local copies, waits for them, and re-layouts  8.72 us

profile of v2, /device:TPU:0, one launch (start us, length us, event | category | flops | bytes accessed | tf_op | source)
XLA Modules:
  0.0 95.9 jit_solution(17885210312503557732)
XLA Ops:
  1.3 34.2 %front.1 = (bf16[6144,512]{1,0:T(8,128)(2,1)}, bf16[512,256]{1,0:T(8,128)(2,1)}, f32[24,256]{1,0:T(8,128)}, bf16[4,8,24,256]{3,2,1,0:T(8,128)(2,1)}, bf16[8,4,24...) custom-call(s32[1]{0:T(128)S(6)} %copy.22.len_ref, bf16[6144,256]{1,0:T(8,128)(2,1)} %bitcast.4, ...), custom_call_target="tpu_custom_call" | custom-call | tf_op jit(solution)/shard_map/front/pallas_call | solution.py:284
  35.5 51.6 %back.1 = (bf16[24,1024]{1,0:T(8,128)(2,1)}, bf16[6144,256]{1,0:T(8,128)(2,1)}, f32[128,512]{1,0:T(8,128)}, f32[64,256]{1,0:T(8,128)}, f32[64,1024]{1,0:T(8,128)...) custom-call(s32[1]{0:T(128)S(6)} %copy.22.len_ref, s32[4,8,128]{2,1,0:T(8,128)} %get-tuple-element.21.lens_ref, ...), custom_call_target="tpu_custom_call" | custom-call | tf_op jit(solution)/shard_map/back/pallas_call | solution.py:730
  87.1 1.4 %copy.23 = bf16[1,24,1024]{2,1,0:T(8,128)(2,1)} copy(bf16[1,24,1024]{2,1,0:T(8,128)(2,1)} %bitcast.9) | data formatting | bytes 98304
  88.5 0.0 copy-start.2
  88.5 0.0 copy-start.4
  88.5 0.0 copy-start.1
  88.5 0.0 copy-start
  88.5 0.0 copy-start.3
  88.6 3.8 %copy.24 = bf16[1,6144,256]{2,1,0:T(8,128)(2,1)} copy(bf16[1,6144,256]{2,1,0:T(8,128)(2,1)} %bitcast.6) | data formatting | bytes 6291456
  92.4 0.0 copy-done.2
  92.4 0.7 copy.25
  93.1 0.0 copy-done.4
  93.1 0.6 copy.26
  93.7 0.0 copy-done.1
  93.7 0.7 copy.27
  94.4 0.0 copy-done
  94.4 0.7 copy.28
  95.2 0.0 copy-done.3
  95.2 0.7 copy.29
Async XLA Ops:
  88.5 3.9 %copy-start.2 = (f32[128,512]{1,0:T(8,128)S(1)}, f32[128,512]{1,0:T(8,128)}, u32[]{:S(2)}) copy-start(f32[128,512]{1,0:T(8,128)} %get-tuple-element.44) | copy-start | bytes 786436
  88.5 4.6 %copy-start.4 = (f32[64,256]{1,0:T(8,128)S(1)}, f32[64,256]{1,0:T(8,128)}, u32[]{:S(2)}) copy-start(f32[64,256]{1,0:T(8,128)} %get-tuple-element.45) | copy-start | bytes 196612
  88.5 5.2 %copy-start.1 = (f32[64,1024]{1,0:T(8,128)S(1)}, f32[64,1024]{1,0:T(8,128)}, u32[]{:S(2)}) copy-start(f32[64,1024]{1,0:T(8,128)} %get-tuple-element.46) | copy-start | bytes 786436
  88.5 5.9 %copy-start = (f32[128,768]{1,0:T(8,128)S(1)}, f32[128,768]{1,0:T(8,128)}, u32[]{:S(2)}) copy-start(f32[128,768]{1,0:T(8,128)} %get-tuple-element.47) | copy-start | bytes 1179652
  88.5 6.7 %copy-start.3 = (f32[256,128]{1,0:T(8,128)S(1)}, f32[256,128]{1,0:T(8,128)}, u32[]{:S(2)}) copy-start(f32[256,128]{1,0:T(8,128)} %get-tuple-element.48) | copy-start | bytes 393220

commit v3 on v2

--- a/solution.py
+++ b/solution.py
@@ -23,9 +23,9 @@
 
 
 def front_kernel(
-    steps, group, len_ref, sig_hbm, w_ref, wout_ref, wres_ref, wgrad_ref,
-    a_hbm, edge_hbm, hsum_ref, pool_ref, ctx_ref, cols_ref, lens_ref,
-    sig, a_buf, grads, gate_w, ctx_mine, cols_mine, sums, sem_in, sem_out, send_tm, recv_tm,
+    steps, group, len_ref, sig_hbm, wqkv_hbm, w_ref, wout_ref, wres_ref, wgrad_ref,
+    a_hbm, edge_hbm, hsum_ref, pool_ref, ctx_ref, cols_ref, lens_ref, wt_ref, wqkvt_ref,
+    sig, a_buf, grads, grads_f, wqkv, gate_w, ctx_mine, cols_mine, sums, sem_in, sem_out, send_tm, recv_tm,
     send_st, recv_st, send_pool, recv_pool, send_near, recv_near, keep,
 ):
     tms, parts = lax.axis_size("tm"), lax.axis_size("stream")
@@ -64,6 +64,8 @@
 
     for i in reversed(range(steps)):
         load(i).start()
+    fetch = pltpu.make_async_copy(wqkv_hbm, wqkv, keep.at[4])
+    fetch.start()
     gate_w[...] = w_ref[:, chans:] * jnp.asarray(0.5, BF16)
 
     halo = pltpu.make_async_remote_copy(
@@ -94,32 +96,44 @@
         )
     ]
 
-    def to_tm(j, d, src, dst):
+    def to_tm(j, d, src, dst, device):
         return pltpu.make_async_remote_copy(
             src_ref=src,
             dst_ref=dst,
             send_sem=send_tm.at[j, d - 1],
             recv_sem=recv_tm.at[j, d - 1],
-            device_id={"tm": lax.rem(tm + d, tms)},
+            device_id=device,
             device_id_type=MESH,
         )
 
     width = grads.shape[2]
     columns = width // tms
 
-    tm_copies = [
-        copy
+    pairs = tms // 2
+    across = {"tm": tm + 1 - 2 * lax.rem(tm, 2)}
+    ctx_copies = [
+        to_tm(0, d, ctx_mine, ctx_ref.at[tm], {"tm": lax.rem(tm + 2 * d, tms)})
+        for d in range(1, pairs)
+    ]
+    ctx_passes = []
+    for d in range(pairs):
+        block = ctx_ref.at[lax.rem(tm - 2 * d + tms, tms)]
+        ctx_passes.append(to_tm(0, pairs + d, block if d else ctx_mine, block, across))
+    cols_copies = [
+        to_tm(
+            1, d, cols_mine.at[lax.rem(tm + d, tms)], cols_ref.at[st, tm],
+            {"tm": lax.rem(tm + d, tms)},
+        )
         for d in range(1, tms)
-        for copy in (
-            to_tm(0, d, ctx_mine, ctx_ref.at[tm]),
-            to_tm(1, d, cols_mine.at[lax.rem(tm + d, tms)], cols_ref.at[tm]),
-        )
     ]
+    cols_shares = [to_stream(2, d, cols_ref.at[st], cols_ref.at[st]) for d in range(1, parts)]
     own_grad = pltpu.make_async_copy(wgrad_ref, grads.at[st], keep.at[0])
     own_ctx = pltpu.make_async_copy(ctx_mine, ctx_ref.at[tm], keep.at[1])
-    own_cols = pltpu.make_async_copy(cols_mine.at[tm], cols_ref.at[tm], keep.at[2])
+    own_cols = pltpu.make_async_copy(cols_mine.at[tm], cols_ref.at[st, tm], keep.at[2])
     edge = pltpu.make_async_copy(sig.at[pl.ds(0, tile)], edge_hbm, keep.at[3])
 
+    for k in range(tms):
+        cols_mine[k] = wgrad_ref[:, k * columns : (k + 1) * columns]
     lens_ref[st] = jnp.full(lens_ref.shape[1:], len_ref[0], jnp.int32)
     length = len_ref[0]
 
@@ -180,7 +194,8 @@
             def _():
                 halo.start()
             own_grad.start()
-            for copy in grad_copies:
+            own_cols.start()
+            for copy in grad_copies + cols_copies:
                 copy.start()
 
         @pl.when(it == 1)
@@ -189,14 +204,23 @@
             for copy in grad_copies:
                 copy.wait()
             for p in range(parts):
-                ctx_mine[p] = lax.dot_general(
-                    grads[p], wout_ref[...], (((1,), (1,)), ((), ())), preferred_element_type=F32
-                ).astype(BF16)
-                for k in range(tms):
-                    cols_mine[k, p] = grads[p, :, k * columns : (k + 1) * columns]
+                grads_f[p * toks : (p + 1) * toks, :] = grads[p].astype(F32)
+            d_ctx = lax.dot_general(
+                grads_f[...].astype(BF16),
+                wout_ref[...],
+                (((1,), (1,)), ((), ())),
+                preferred_element_type=F32,
+            )
+            for p in range(parts):
+                ctx_mine[p] = d_ctx[p * toks : (p + 1) * toks, :].astype(BF16)
             own_ctx.start()
-            own_cols.start()
-            for copy in tm_copies:
+            for copy in ctx_copies:
+                copy.start()
+            ctx_passes[0].start()
+            own_cols.wait()
+            for copy in cols_copies:
+                copy.wait()
+            for copy in cols_shares:
                 copy.start()
 
         return carry
@@ -253,11 +277,18 @@
 
     lax.fori_loop(1, others, launch, 0)
     relay(0).start()
+    wt_ref[...] = w_ref[...].T
+    fetch.wait()
+    wqkvt_ref[...] = wqkv[...].T
+    for copy, onward in zip(ctx_copies, ctx_passes[1:]):
+        copy.wait_recv()
+        onward.start()
     lax.fori_loop(1, others, forward, 0)
-    for copy in tm_copies:
+    for copy in ctx_copies:
+        copy.wait_send()
+    for copy in ctx_passes + cols_shares:
         copy.wait()
     own_ctx.wait()
-    own_cols.wait()
     edge.wait()
     for i in range(steps):
         save(i).wait()
@@ -270,7 +301,7 @@
     lax.fori_loop(0, others, close, 0)
 
 
-def front(lengths, signal, w_conv, w_out, w_res, d_out, collective):
+def front(lengths, signal, w_qkv, w_conv, w_out, w_res, d_out, collective):
     samples, chans = signal.shape
     toks, width = d_out.shape
     tms, parts = lax.axis_size("tm"), lax.axis_size("stream")
@@ -289,34 +320,38 @@
             jax.ShapeDtypeStruct((toks, chans), F32),
             jax.ShapeDtypeStruct((parts, tms, toks, chans), BF16),
             jax.ShapeDtypeStruct((tms, parts, toks, inner), BF16),
-            jax.ShapeDtypeStruct((tms, parts, toks, columns), BF16),
+            jax.ShapeDtypeStruct((parts, tms, toks, columns), BF16),
             jax.ShapeDtypeStruct((parts, 8, 128), jnp.int32),
+            jax.ShapeDtypeStruct(w_conv.shape[::-1], BF16),
+            jax.ShapeDtypeStruct(w_qkv.shape[::-1], BF16),
         ],
-        in_specs=[pl.BlockSpec(memory_space=pltpu.SMEM), anywhere] + [VMEM_SPEC] * 4,
-        out_specs=[anywhere, anywhere] + [VMEM_SPEC] * 5,
+        in_specs=[pl.BlockSpec(memory_space=pltpu.SMEM), anywhere, anywhere] + [VMEM_SPEC] * 4,
+        out_specs=[anywhere, anywhere] + [VMEM_SPEC] * 7,
         scratch_shapes=[
             pltpu.VMEM((samples + DILATION_STEP, chans), BF16),
             pltpu.VMEM((samples, 2 * chans), BF16),
             pltpu.VMEM((parts, toks, width), BF16),
+            pltpu.VMEM((parts * toks, width), F32),
+            pltpu.VMEM(w_qkv.shape, BF16),
             pltpu.VMEM((2 * chans, chans), BF16),
             pltpu.VMEM((parts, toks, inner), BF16),
-            pltpu.VMEM((tms, parts, toks, columns), BF16),
+            pltpu.VMEM((tms, toks, columns), BF16),
             pltpu.VMEM((toks, chans), F32),
             dma((steps,)),
             dma((steps,)),
             dma((3, tms - 1)),
             dma((3, tms - 1)),
-            dma((2, parts - 1)),
-            dma((2, parts - 1)),
+            dma((3, parts - 1)),
+            dma((3, parts - 1)),
             dma((others,)),
             dma((others,)),
             dma((others,)),
             dma((others,)),
-            dma((4,)),
+            dma((5,)),
         ],
         compiler_params=pltpu.CompilerParams(collective_id=collective, has_side_effects=True),
         name="front",
-    )(lengths, signal, w_conv, w_out, w_res, d_out)
+    )(lengths, signal, w_qkv, w_conv, w_out, w_res, d_out)
 
 
 NT = (((1,), (1,)), ((), ()))
@@ -359,13 +394,13 @@
 
 def back_kernel(
     steps, heads, len_ref, lens_ref, sig_hbm, edge_hbm, a_hbm, hsum_ref, pool_ref, ctx_in, cols_in,
-    w_ref, wres_ref, win_ref, wqkv_ref, wout_ref, grad_ref,
+    wt_ref, wres_ref, win_ref, wqkv_ref, wqkvt_ref, wout_ref, grad_ref,
     out_ref, dsig_hbm, gconv_ref, gres_ref, gin_ref, gqkv_ref, gout_ref,
     sig, a_buf, dsig, first, arrive, pool_f, pool_b, dctx_f, dctx_b, cols_f, cols_b, tok_v, norm,
     proj, ctx_v, dproj, dg, gin_acc, cols_acc, own_send, own_land, out_send, out_land, cols_mine,
     cols_land, in_parts, in_near, in_sum, in_far, conv_acc, conv_parts, conv_near, conv_sum,
     conv_far, conv_f, conv_rows, conv_rland, conv_own, conv_land, res_acc, res_parts, res_near,
-    res_sum, res_far, res_f, res_rows, res_rland, res_own, res_land, dh8, dr8,
+    res_sum, res_far, res_f, res_rows, res_rland, res_own, res_land, dh8, dr8, turned,
     sem_in, sem_a, sem_out, send, recv,
 ):
     tms, parts = lax.axis_size("tm"), lax.axis_size("stream")
@@ -374,7 +409,7 @@
     core, chip = lax.rem(st, 2), st // 2
     tile = DILATION_STEP
     samples = steps * tile
-    chans = w_ref.shape[1] // 2
+    chans = wt_ref.shape[1] // 2
     toks, width = grad_ref.shape
     total = tms * toks
     inner = wout_ref.shape[0]
@@ -443,7 +478,7 @@
             rows = slice(k * toks, (k + 1) * toks)
             pool_f[rows, :] = pool_ref[s, k].astype(F32)
             dctx_f[rows, :] = ctx_in[k, s].astype(F32)
-            cols_f[rows, :] = cols_in[k, s].astype(F32)
+            cols_f[rows, :] = cols_in[s, k].astype(F32)
         pool_b[...] = pool_f[...].astype(BF16)
         dctx_b[...] = dctx_f[...].astype(BF16)
         cols_b[...] = cols_f[...].astype(BF16)
@@ -469,7 +504,7 @@
                     own = norm[:, k * columns : (k + 1) * columns]
                     gqkv_ref[...] += fdot(own, dproj[...], TN)
 
-        d_normed = fdot(dproj[...], wqkv_ref[...], NT)
+        d_normed = fdot(dproj[...], wqkvt_ref[...])
         tok = tok_v[...]
         along = jnp.sum(d_normed * tok, axis=-1, keepdims=True)
         d_group = r * d_normed - tok * (r * r * r * along / width)
@@ -586,9 +621,10 @@
     per_tile = tile // POOL
 
     def later_of(i):
-        return fdot(a_buf[pl.ds(i * tile, tile), :], w_ref[:chans, :], NT).astype(BF16)
+        return fdot(a_buf[pl.ds(i * tile, tile), :], wt_ref[:, :chans]).astype(BF16)
 
     conv_acc[...] = jnp.zeros_like(conv_acc)
+    turned[:chans, :] = sig[pl.ds(0, tile), :].T
 
     def weigh(i, carry):
         rows = pl.ds(i * tile, tile)
@@ -601,8 +637,9 @@
                 a = a_buf[base, lanes].astype(F32).reshape(POOL // 8, 8, chans)
                 a_buf[base, lanes] = (a * gate[None]).reshape(POOL, chans).astype(BF16)
         dm = a_buf[rows, :]
-        conv_acc[:chans, :] += fdot(sig[rows, :], dm, TN)
-        conv_acc[chans:, :] += fdot(sig[pl.ds((i + 1) * tile, tile), :], dm, TN)
+        turned[chans:, :] = sig[pl.ds((i + 1) * tile, tile), :].T
+        conv_acc[...] += fdot(turned[...], dm)
+        turned[:chans, :] = turned[chans:, :]
 
         @pl.when(i == 0)
         def _():
@@ -623,7 +660,7 @@
 
     def emit(i, later):
         rows = pl.ds(i * tile, tile)
-        here = fdot(a_buf[rows, :], w_ref[chans:, :], NT)
+        here = fdot(a_buf[rows, :], wt_ref[:, chans:])
         for j in range(per_tile):
             token = i * per_tile + j
             index = lax.broadcasted_iota(jnp.int32, (POOL, 128), 0) + (tm * samples + token * POOL)
@@ -694,7 +731,7 @@
 
 
 def back(lengths, lens, signal, edge, gates, hsum, pool, ctx, cols, weights, d_out, heads, collective):
-    w_conv, w_res, w_in, w_qkv, w_out = weights
+    w_convt, w_res, w_in, w_qkv, w_qkvt, w_out = weights
     samples, chans = signal.shape
     toks, width = d_out.shape
     tms, parts = lax.axis_size("tm"), lax.axis_size("stream")
@@ -739,7 +776,7 @@
             jax.ShapeDtypeStruct((inner, columns), F32),
         ],
         in_specs=[pl.BlockSpec(memory_space=pltpu.SMEM), VMEM_SPEC, anywhere, anywhere, anywhere]
-        + [VMEM_SPEC] * 10,
+        + [VMEM_SPEC] * 11,
         out_specs=[VMEM_SPEC, anywhere] + [VMEM_SPEC] * 5,
         scratch_shapes=[
             vm(samples + DILATION_STEP, chans),
@@ -777,6 +814,7 @@
         + [
             vm(toks, 8, chans, dtype=F32),
             vm(toks, 8, chans, dtype=F32),
+            vm(joined, DILATION_STEP),
             dma((2,)),
             dma((1,)),
             dma((steps,)),
@@ -787,7 +825,45 @@
             collective_id=collective, has_side_effects=True, vmem_limit_bytes=60 * 1024 * 1024
         ),
         name="back",
-    )(lengths, lens, signal, edge, gates, hsum, pool, ctx, cols, w_conv, w_res, w_in, w_qkv, w_out, d_out)
+    )(lengths, lens, signal, edge, gates, hsum, pool, ctx, cols, *weights, d_out)
+
+
+def hand_kernel(cuts, *refs):
+    n = len(cuts)
+    ins, outs, bufs, (sem_in, sem_out) = refs[:n], refs[n : 2 * n], refs[2 * n : 3 * n], refs[3 * n :]
+    pulls, pushes = [], []
+    for j, pieces in enumerate(cuts):
+        rows = ins[j].shape[0] // pieces
+        for k in range(pieces):
+            part = pl.ds(k * rows, rows)
+            at = len(pulls)
+            pulls.append(
+                pltpu.make_async_copy(ins[j].at[part], bufs[j].at[part], sem_in.at[at])
+            )
+            pushes.append(
+                pltpu.make_async_copy(bufs[j].at[part], outs[j].at[part], sem_out.at[at])
+            )
+    for copy in pulls:
+        copy.start()
+    for pull, push in zip(pulls, pushes):
+        pull.wait()
+        push.start()
+    for copy in pushes:
+        copy.wait()
+
+
+def hand(arrays, cuts):
+    anywhere = pl.BlockSpec(memory_space=pl.ANY)
+    return pl.pallas_call(
+        functools.partial(hand_kernel, cuts),
+        out_shape=[jax.ShapeDtypeStruct(a.shape, a.dtype) for a in arrays],
+        in_specs=[anywhere] * len(arrays),
+        out_specs=[anywhere] * len(arrays),
+        scratch_shapes=[pltpu.VMEM(a.shape, a.dtype) for a in arrays]
+        + [pltpu.SemaphoreType.DMA((sum(cuts),))] * 2,
+        compiler_params=pltpu.CompilerParams(vmem_limit_bytes=60 * 1024 * 1024),
+        name="hand",
+    )(*arrays)
 
 
 def local(signal, lengths, w_conv, w_res, w_in, w_qkv, w_out, d_out):
@@ -795,13 +871,14 @@
     toks, width = d_out.shape[1:]
     flat, grad = signal.reshape(samples, chans), d_out.reshape(toks, width)
     heads = w_out.shape[0] // (width // HEADS)
-    gates, edge, hsum, pool, ctx, cols, lens = front(
-        lengths, flat, w_conv, w_out, w_res, grad, 0
+    gates, edge, hsum, pool, ctx, cols, lens, w_convt, w_qkvt = front(
+        lengths, flat, w_qkv, w_conv, w_out, w_res, grad, 0
     )
-    weights = (w_conv, w_res, w_in, w_qkv, w_out)
-    out, d_sig, *grads = back(
+    weights = (w_convt, w_res, w_in, w_qkv, w_qkvt, w_out)
+    results = back(
         lengths, lens, flat, edge, gates, hsum, pool, ctx, cols, weights, grad, heads, 1
     )
+    out, d_sig, *grads = hand(results, (1, 12, 1, 1, 1, 1, 1))
     return (out[None], d_sig[None], *grads)
 
 

time: 96.1 us -> 84.5 us (0.88)
  local copies, waits for them, and re-layouts: 8.72 us -> 0 us
  Pallas kernels: 85.8 us -> 83 us
    unnamed x17 -> x0, local copies, waits for them, and re-layouts: 8.72 us -> none
    pallas_call x1, Pallas kernels: 34.2 us -> 29 us  [front(): pl.pallas_call(functools.partial(front_kernel, steps, group), out_shape=[...]
    pallas_call x0 -> x1, Pallas kernels: none -> 3.98 us  [hand(): pl.pallas_call(functools.partial(hand_kernel, cuts), out_shape=[jax.Shape...]
    pallas_call x1, Pallas kernels: 51.6 us -> 50.1 us  [back(): pl.pallas_call(functools.partial(back_kernel, steps, heads), out_shape=[j...]
where the time goes in v3:
time: 84.5 us; the launch traced here: 84.3 us
  Pallas kernels  83 us (98%)
  between operations  1.29 us (2%)
    pallas_call x1, Pallas kernels, back(): pl.pallas_call(functools.partial(back_kernel, steps, heads), out_shape=[j...  50.1 us
    pallas_call x1, Pallas kernels, front(): pl.pallas_call(functools.partial(front_kernel, steps, group), out_shape=[...  29 us
    pallas_call x1, Pallas kernels, hand(): pl.pallas_call(functools.partial(hand_kernel, cuts), out_shape=[jax.Shape...  3.98 us

profile of v3, /device:TPU:0, one launch (start us, length us, event | category | flops | bytes accessed | tf_op | source)
XLA Modules:
  0.0 84.3 jit_solution(4350570561656036280)
XLA Ops:
  1.3 29.0 %front.1 = (bf16[6144,512]{1,0:T(8,128)(2,1)}, bf16[512,256]{1,0:T(8,128)(2,1)}, f32[24,256]{1,0:T(8,128)}, bf16[4,8,24,256]{3,2,1,0:T(8,128)(2,1)}, bf16[8,4,24...) custom-call(s32[1]{0:T(128)S(6)} %copy.15.len_ref, ...), custom_call_target="tpu_custom_call" | custom-call | tf_op jit(solution)/shard_map/front/pallas_call | solution.py:315
  30.2 50.1 %back.1 = (bf16[24,1024]{1,0:T(8,128)(2,1)}, bf16[6144,256]{1,0:T(8,128)(2,1)}, f32[128,512]{1,0:T(8,128)}, f32[64,256]{1,0:T(8,128)}, f32[64,1024]{1,0:T(8,128)...) custom-call(s32[1]{0:T(128)S(6)} %copy.15.len_ref, s32[4,8,128]{2,1,0:T(8,128)} %get-tuple-element.30.lens_ref, ...), custom_call_target="tpu_custom_call" | custom-call | tf_op jit(solution)/shard_map/back/pallas_call | solution.py:767
  80.3 4.0 %hand.1 = (bf16[24,1024]{1,0:T(8,128)(2,1)}, bf16[6144,256]{1,0:T(8,128)(2,1)}, f32[128,512]{1,0:T(8,128)}, f32[64,256]{1,0:T(8,128)}, f32[64,1024]{1,0:T(8,128)...) custom-call(bf16[24,1024]{1,0:T(8,128)(2,1)} %get-tuple-element.39.refs_0_, bf16[6144,256]{1,0:T(8,128)(2,1)} %get-tuple-element.40.refs_1_, ...), custom_call_target="tpu_custom_call" | custom-call | tf_op jit(solution)/shard_map/hand/pallas_call | solution.py:857

commit v4 on v3

--- a/solution.py
+++ b/solution.py
@@ -185,18 +185,6 @@
         block = pl.ds(pl.multiple_of(r * group * per_tile, 8), group * per_tile)
         hsum_ref[block, :] = jnp.concatenate([a for a, _ in rows], axis=0)
         sums[block, :] = jnp.concatenate([b for _, b in rows], axis=0)
-
-        @pl.when(it == 0)
-        def _():
-            pl.semaphore_wait(barrier, others - 1 + chips)
-
-            @pl.when(tm < tms - 1)
-            def _():
-                halo.start()
-            own_grad.start()
-            own_cols.start()
-            for copy in grad_copies + cols_copies:
-                copy.start()
 
         @pl.when(it == 1)
         def _():
@@ -225,6 +213,16 @@
 
         return carry
 
+    pl.semaphore_wait(barrier, others - 1 + chips)
+
+    @pl.when(tm < tms - 1)
+    def _():
+        halo.start()
+
+    own_grad.start()
+    own_cols.start()
+    for copy in grad_copies + cols_copies:
+        copy.start()
     load(steps - 1).wait()
     lax.fori_loop(0, rounds, body, 0)
     edge.start()
@@ -400,7 +398,7 @@
     proj, ctx_v, dproj, dg, gin_acc, cols_acc, own_send, own_land, out_send, out_land, cols_mine,
     cols_land, in_parts, in_near, in_sum, in_far, conv_acc, conv_parts, conv_near, conv_sum,
     conv_far, conv_f, conv_rows, conv_rland, conv_own, conv_land, res_acc, res_parts, res_near,
-    res_sum, res_far, res_f, res_rows, res_rland, res_own, res_land, dh8, dr8, turned,
+    res_sum, res_far, res_f, res_rows, res_rland, res_own, res_land, dh8, dr8, turned, rate,
     sem_in, sem_a, sem_out, send, recv,
 ):
     tms, parts = lax.axis_size("tm"), lax.axis_size("stream")
@@ -471,28 +469,65 @@
     gqkv_ref[...] = jnp.zeros_like(gqkv_ref)
     gin_acc[...] = jnp.zeros_like(gin_acc)
     cols_acc[...] = jnp.zeros_like(cols_acc)
-    mine = pl.ds(pl.multiple_of(tm * toks, 8), toks)
-
-    def stay(s, carry):
-        for k in range(tms):
-            rows = slice(k * toks, (k + 1) * toks)
-            pool_f[rows, :] = pool_ref[s, k].astype(F32)
-            dctx_f[rows, :] = ctx_in[k, s].astype(F32)
-            cols_f[rows, :] = cols_in[s, k].astype(F32)
+    batch = pool_b.shape[0] // total
+
+    def lead(b):
+        for s in range(batch):
+            for k in range(tms):
+                rows = slice(s * total + k * toks, s * total + (k + 1) * toks)
+                pool_f[rows, :] = pool_ref[b * batch + s, k].astype(F32)
+                dctx_f[rows, :] = ctx_in[k, b * batch + s].astype(F32)
+                cols_f[rows, :] = cols_in[b * batch + s, k].astype(F32)
         pool_b[...] = pool_f[...].astype(BF16)
         dctx_b[...] = dctx_f[...].astype(BF16)
         cols_b[...] = cols_f[...].astype(BF16)
-        tok = fdot(pool_b[...], win_ref[...]).astype(BF16).astype(F32)
-        tok_v[...] = tok
-        r = lax.rsqrt(jnp.mean(tok * tok, axis=-1, keepdims=True) + EPS)
-        norm[...] = (tok * r).astype(BF16)
+        tok_v[...] = fdot(pool_b[...], win_ref[...]).astype(BF16).astype(F32)
+
+        def scaled(s, c):
+            rows = pl.ds(pl.multiple_of(s * total, total), total)
+            tok = tok_v[rows, :]
+            r = lax.rsqrt(jnp.mean(tok * tok, axis=-1, keepdims=True) + EPS)
+            norm[rows, :] = (tok * r).astype(BF16)
+            rate[rows, :] = jnp.broadcast_to(r, (total, 128))
+            return c
+
+        lax.fori_loop(0, batch, scaled, 0)
         proj[...] = fdot(norm[...], wqkv_ref[...]).astype(BF16)
-        limit = lens_ref[s, 0:1, 0:1]
-        allowed = (col <= row) & (col * POOL < limit)
-        attend(heads, size, allowed, proj, dctx_b, ctx_v, dproj)
-        context = ctx_v[...].astype(BF16)
-        gout_ref[...] += fdot(context, cols_b[...], TN)
+
+        def look(s, c):
+            rows = pl.ds(pl.multiple_of(s * total, total), total)
+            limit = lens_ref[b * batch + s, 0:1, 0:1]
+            allowed = (col <= row) & (col * POOL < limit)
+            attend(
+                heads, size, allowed, proj.at[rows], dctx_b.at[rows], ctx_v.at[rows], dproj.at[rows]
+            )
+            return c
+
+        lax.fori_loop(0, batch, look, 0)
+        dg[...] = fdot(dproj[...], wqkvt_ref[...])
+
+        def through(s, c):
+            rows = pl.ds(pl.multiple_of(s * total, total), total)
+            own = pl.ds(pl.multiple_of(s * total + tm * toks, 8), toks)
+            d_normed, tok = dg[rows, :], tok_v[rows, :]
+            r = rate[rows, 0:1]
+            along = jnp.sum(d_normed * tok, axis=-1, keepdims=True)
+            dg[rows, :] = r * d_normed - tok * (r * r * r * along / width)
+            own_send[b * batch + s] = dg[own, :].astype(BF16)
+            return c
+
+        lax.fori_loop(0, batch, through, 0)
+
+    def follow(b):
+        for s in range(batch):
+            own = pl.ds(pl.multiple_of(s * total + tm * toks, 8), toks)
+            value = fdot(ctx_v[own, :].astype(BF16), wout_ref[...])
+            out_send[b * batch + s] = value.astype(BF16)
+        gin_acc[...] += fdot(pool_b[...], dg[...].astype(BF16), TN)
         cols_acc[...] += fdot(pool_b[...], cols_b[...], TN)
+
+    def weights(b):
+        gout_ref[...] += fdot(ctx_v[...].astype(BF16), cols_b[...], TN)
         if columns % 128 == 0:
             own = norm[:, pl.ds(pl.multiple_of(tm * columns, columns), columns)]
             gqkv_ref[...] += fdot(own, dproj[...], TN)
@@ -504,17 +539,17 @@
                     own = norm[:, k * columns : (k + 1) * columns]
                     gqkv_ref[...] += fdot(own, dproj[...], TN)
 
-        d_normed = fdot(dproj[...], wqkvt_ref[...])
-        tok = tok_v[...]
-        along = jnp.sum(d_normed * tok, axis=-1, keepdims=True)
-        d_group = r * d_normed - tok * (r * r * r * along / width)
-        dg[...] = d_group
-        own_send[s] = dg[mine, :].astype(BF16)
-        out_send[s] = fdot(ctx_v[mine, :].astype(BF16), wout_ref[...]).astype(BF16)
-        gin_acc[...] += fdot(pool_b[...], d_group.astype(BF16), TN)
-        return carry
-
-    lax.fori_loop(0, parts, stay, 0)
+    batches = parts // batch
+
+    def whole_batch(b, c):
+        lead(b)
+        follow(b)
+        weights(b)
+        return c
+
+    if batches > 1:
+        lax.fori_loop(0, batches - 1, whole_batch, 0)
+    lead(batches - 1)
 
     own_copies = [
         remote(own_send.at[lax.rem(st + d, parts)], own_land.at[d - 1], to_stream(d))
@@ -589,6 +624,7 @@
 
     pl.semaphore_wait(barrier, parts - 1 + tms - 1)
     begin(own_copies)
+    follow(batches - 1)
     split(gin_acc, in_parts)
     cols_mine[...] = cols_acc[pl.ds(pl.multiple_of(st * in_rows, 8), in_rows), :].astype(BF16)
     cols_land[tm] = cols_mine[...]
@@ -655,6 +691,7 @@
 
     split(conv_acc, conv_parts)
     begin(conv_one)
+    weights(batches - 1)
 
     length = len_ref[0]
 
@@ -738,6 +775,7 @@
     chips = parts // 2
     steps = samples // DILATION_STEP
     total = toks * tms
+    rows = total * max(n for n in range(1, parts + 1) if parts % n == 0 and (n == 1 or n * total <= 768))
     inner = w_out.shape[0]
     triple = w_qkv.shape[1]
     columns = width // tms
@@ -749,9 +787,9 @@
     def vm(*shape, dtype=BF16):
         return pltpu.VMEM(shape, dtype)
 
-    def reduction(rows, n, lanes):
+    def reduction(size, n, lanes):
         return [
-            vm(rows, lanes, dtype=F32),
+            vm(size, lanes, dtype=F32),
             vm(2, chips, n, lanes),
             vm(chips, n, lanes),
             vm(chips, n, lanes),
@@ -784,18 +822,18 @@
             vm(samples, chans),
             vm(DILATION_STEP, chans),
             vm(DILATION_STEP, chans),
-            vm(total, chans, dtype=F32),
-            vm(total, chans),
-            vm(total, inner, dtype=F32),
-            vm(total, inner),
-            vm(total, columns, dtype=F32),
-            vm(total, columns),
-            vm(total, width, dtype=F32),
-            vm(total, width),
-            vm(total, triple),
-            vm(total, inner, dtype=F32),
-            vm(total, triple),
-            vm(total, width, dtype=F32),
+            vm(rows, chans, dtype=F32),
+            vm(rows, chans),
+            vm(rows, inner, dtype=F32),
+            vm(rows, inner),
+            vm(rows, columns, dtype=F32),
+            vm(rows, columns),
+            vm(rows, width, dtype=F32),
+            vm(rows, width),
+            vm(rows, triple),
+            vm(rows, inner, dtype=F32),
+            vm(rows, triple),
+            vm(rows, width, dtype=F32),
             vm(chans, width, dtype=F32),
             vm(chans, columns, dtype=F32),
             vm(parts, toks, width),
@@ -815,6 +853,7 @@
             vm(toks, 8, chans, dtype=F32),
             vm(toks, 8, chans, dtype=F32),
             vm(joined, DILATION_STEP),
+            vm(rows, 128, dtype=F32),
             dma((2,)),
             dma((1,)),
             dma((steps,)),
@@ -878,7 +917,7 @@
     results = back(
         lengths, lens, flat, edge, gates, hsum, pool, ctx, cols, weights, grad, heads, 1
     )
-    out, d_sig, *grads = hand(results, (1, 12, 1, 1, 1, 1, 1))
+    out, d_sig, *grads = hand(results, (1, 3, 1, 1, 1, 1, 1))
     return (out[None], d_sig[None], *grads)
 
 

time: 84.5 us -> 79.9 us (0.946)
  Pallas kernels: 83 us -> 78.4 us
    pallas_call x1, Pallas kernels: 50.1 us -> 46.5 us  [back(): pl.pallas_call(functools.partial(back_kernel, steps, heads), out_shape=[j...]
where the time goes in v4:
time: 79.9 us; the launch traced here: 79.7 us
  Pallas kernels  78.4 us (98%)
  between operations  1.29 us (2%)
    pallas_call x1, Pallas kernels, back(): pl.pallas_call(functools.partial(back_kernel, steps, heads), out_shape=[j...  46.5 us
    pallas_call x1, Pallas kernels, front(): pl.pallas_call(functools.partial(front_kernel, steps, group), out_shape=[...  28.5 us
    pallas_call x1, Pallas kernels, hand(): pl.pallas_call(functools.partial(hand_kernel, cuts), out_shape=[jax.Shape...  3.43 us

profile of v4, /device:TPU:0, one launch (start us, length us, event | category | flops | bytes accessed | tf_op | source)
XLA Modules:
  0.0 79.7 jit_solution(384906499698681016)
XLA Ops:
  1.3 28.5 %front.1 = (bf16[6144,512]{1,0:T(8,128)(2,1)}, bf16[512,256]{1,0:T(8,128)(2,1)}, f32[24,256]{1,0:T(8,128)}, bf16[4,8,24,256]{3,2,1,0:T(8,128)(2,1)}, bf16[8,4,24...) custom-call(s32[1]{0:T(128)S(6)} %copy.15.len_ref, ...), custom_call_target="tpu_custom_call" | custom-call | tf_op jit(solution)/shard_map/front/pallas_call | solution.py:313
  29.8 46.5 %back.1 = (bf16[24,1024]{1,0:T(8,128)(2,1)}, bf16[6144,256]{1,0:T(8,128)(2,1)}, f32[128,512]{1,0:T(8,128)}, f32[64,256]{1,0:T(8,128)}, f32[64,1024]{1,0:T(8,128)...) custom-call(s32[1]{0:T(128)S(6)} %copy.15.len_ref, s32[4,8,128]{2,1,0:T(8,128)} %get-tuple-element.30.lens_ref, ...), custom_call_target="tpu_custom_call" | custom-call | tf_op jit(solution)/shard_map/back/pallas_call | solution.py:805
  76.3 3.4 %hand.1 = (bf16[24,1024]{1,0:T(8,128)(2,1)}, bf16[6144,256]{1,0:T(8,128)(2,1)}, f32[128,512]{1,0:T(8,128)}, f32[64,256]{1,0:T(8,128)}, f32[64,1024]{1,0:T(8,128)...) custom-call(bf16[24,1024]{1,0:T(8,128)(2,1)} %get-tuple-element.39.refs_0_, bf16[6144,256]{1,0:T(8,128)(2,1)} %get-tuple-element.40.refs_1_, ...), custom_call_target="tpu_custom_call" | custom-call | tf_op jit(solution)/shard_map/hand/pallas_call | solution.py:896

commit v5 on v4

--- a/solution.py
+++ b/solution.py
@@ -391,14 +391,15 @@
 
 
 def back_kernel(
-    steps, heads, len_ref, lens_ref, sig_hbm, edge_hbm, a_hbm, hsum_ref, pool_ref, ctx_in, cols_in,
-    wt_ref, wres_ref, win_ref, wqkv_ref, wqkvt_ref, wout_ref, grad_ref,
+    steps, heads, len_ref, lens_ref, sig_hbm, edge_hbm, a_hbm, hsum_ref, pool_ref, ctx_hbm, cols_hbm,
+    wt_hbm, wres_ref, win_ref, wqkv_hbm, wqkvt_hbm, wout_hbm, grad_ref,
     out_ref, dsig_hbm, gconv_ref, gres_ref, gin_ref, gqkv_ref, gout_ref,
     sig, a_buf, dsig, first, arrive, pool_f, pool_b, dctx_f, dctx_b, cols_f, cols_b, tok_v, norm,
     proj, ctx_v, dproj, dg, gin_acc, cols_acc, own_send, own_land, out_send, out_land, cols_mine,
     cols_land, in_parts, in_near, in_sum, in_far, conv_acc, conv_parts, conv_near, conv_sum,
     conv_far, conv_f, conv_rows, conv_rland, conv_own, conv_land, res_acc, res_parts, res_near,
     res_sum, res_far, res_f, res_rows, res_rland, res_own, res_land, dh8, dr8, turned, rate,
+    ctx_in, cols_in, wt_ref, wqkv_ref, wqkvt_ref, wout_ref, sem_w,
     sem_in, sem_a, sem_out, send, recv,
 ):
     tms, parts = lax.axis_size("tm"), lax.axis_size("stream")
@@ -425,6 +426,21 @@
             barrier, inc=1, device_id={"tm": lax.rem(tm + d, tms)}, device_id_type=MESH
         )
 
+    names = ("wqkv", "ctx", "cols", "wqkvt", "wout", "wt")
+    sources = (wqkv_hbm, ctx_hbm, cols_hbm, wqkvt_hbm, wout_hbm, wt_hbm)
+    targets = (wqkv_ref, ctx_in, cols_in, wqkvt_ref, wout_ref, wt_ref)
+    pending = {
+        name: pltpu.make_async_copy(src, dst, sem_w.at[k])
+        for k, (name, src, dst) in enumerate(zip(names, sources, targets))
+    }
+    for copy in pending.values():
+        copy.start()
+
+    def need(*wanted):
+        for name in wanted:
+            if name in pending:
+                pending.pop(name).wait()
+
     loads = [pltpu.make_async_copy(edge_hbm, sig.at[pl.ds(0, tile)], sem_in.at[0])]
     loads.append(pltpu.make_async_copy(sig_hbm, sig.at[pl.ds(tile, samples)], sem_in.at[1]))
     loads.append(pltpu.make_async_copy(a_hbm, a_buf, sem_a.at[0]))
@@ -476,11 +492,7 @@
             for k in range(tms):
                 rows = slice(s * total + k * toks, s * total + (k + 1) * toks)
                 pool_f[rows, :] = pool_ref[b * batch + s, k].astype(F32)
-                dctx_f[rows, :] = ctx_in[k, b * batch + s].astype(F32)
-                cols_f[rows, :] = cols_in[b * batch + s, k].astype(F32)
         pool_b[...] = pool_f[...].astype(BF16)
-        dctx_b[...] = dctx_f[...].astype(BF16)
-        cols_b[...] = cols_f[...].astype(BF16)
         tok_v[...] = fdot(pool_b[...], win_ref[...]).astype(BF16).astype(F32)
 
         def scaled(s, c):
@@ -492,7 +504,15 @@
             return c
 
         lax.fori_loop(0, batch, scaled, 0)
+        need("wqkv", "ctx", "cols")
         proj[...] = fdot(norm[...], wqkv_ref[...]).astype(BF16)
+        for s in range(batch):
+            for k in range(tms):
+                rows = slice(s * total + k * toks, s * total + (k + 1) * toks)
+                dctx_f[rows, :] = ctx_in[k, b * batch + s].astype(F32)
+                cols_f[rows, :] = cols_in[b * batch + s, k].astype(F32)
+        dctx_b[...] = dctx_f[...].astype(BF16)
+        cols_b[...] = cols_f[...].astype(BF16)
 
         def look(s, c):
             rows = pl.ds(pl.multiple_of(s * total, total), total)
@@ -504,6 +524,7 @@
             return c
 
         lax.fori_loop(0, batch, look, 0)
+        need("wqkvt")
         dg[...] = fdot(dproj[...], wqkvt_ref[...])
 
         def through(s, c):
@@ -519,6 +540,7 @@
         lax.fori_loop(0, batch, through, 0)
 
     def follow(b):
+        need("wout")
         for s in range(batch):
             own = pl.ds(pl.multiple_of(s * total + tm * toks, 8), toks)
             value = fdot(ctx_v[own, :].astype(BF16), wout_ref[...])
@@ -548,6 +570,7 @@
         return c
 
     if batches > 1:
+        need(*names)
         lax.fori_loop(0, batches - 1, whole_batch, 0)
     lead(batches - 1)
 
@@ -653,6 +676,7 @@
     add_near(in_parts, in_near, in_sum)
     begin(in_two)
     finish(loads)
+    need("wt")
 
     per_tile = tile // POOL
 
@@ -713,7 +737,7 @@
         emit(i, later_of(i + 1))
         return carry
 
-    cuts = [0, steps // 6, steps // 2, steps - 1]
+    cuts = [0, steps // 12, steps // 3, steps - 1]
     lax.fori_loop(cuts[0], cuts[1], emit_step, 0)
     finish(conv_one)
     add_near(conv_parts, conv_near, conv_sum)
@@ -813,8 +837,13 @@
             jax.ShapeDtypeStruct((columns, triple), F32),
             jax.ShapeDtypeStruct((inner, columns), F32),
         ],
-        in_specs=[pl.BlockSpec(memory_space=pltpu.SMEM), VMEM_SPEC, anywhere, anywhere, anywhere]
-        + [VMEM_SPEC] * 11,
+        in_specs=[pl.BlockSpec(memory_space=pltpu.SMEM), VMEM_SPEC]
+        + [anywhere] * 3
+        + [VMEM_SPEC] * 2
+        + [anywhere] * 3
+        + [VMEM_SPEC] * 2
+        + [anywhere] * 3
+        + [VMEM_SPEC],
         out_specs=[VMEM_SPEC, anywhere] + [VMEM_SPEC] * 5,
         scratch_shapes=[
             vm(samples + DILATION_STEP, chans),
@@ -854,6 +883,13 @@
             vm(toks, 8, chans, dtype=F32),
             vm(joined, DILATION_STEP),
             vm(rows, 128, dtype=F32),
+            vm(*ctx.shape),
+            vm(*cols.shape),
+            vm(*w_convt.shape),
+            vm(*w_qkv.shape),
+            vm(*w_qkvt.shape),
+            vm(*w_out.shape),
+            dma((6,)),
             dma((2,)),
             dma((1,)),
             dma((steps,)),

time: 79.9 us -> 78.4 us (0.981)
  Pallas kernels: 78.4 us -> 76.9 us
    pallas_call x1, Pallas kernels: 46.5 us -> 45 us  [back(): pl.pallas_call(functools.partial(back_kernel, steps, heads), out_shape=[j...]
where the time goes in v5:
time: 78.4 us; the launch traced here: 78.2 us
  Pallas kernels  76.9 us (98%)
  between operations  1.29 us (2%)
    pallas_call x1, Pallas kernels, back(): pl.pallas_call(functools.partial(back_kernel, steps, heads), out_shape=[j...  45 us
    pallas_call x1, Pallas kernels, front(): pl.pallas_call(functools.partial(front_kernel, steps, group), out_shape=[...  28.5 us
    pallas_call x1, Pallas kernels, hand(): pl.pallas_call(functools.partial(hand_kernel, cuts), out_shape=[jax.Shape...  3.43 us

profile of v5, /device:TPU:0, one launch (start us, length us, event | category | flops | bytes accessed | tf_op | source)
XLA Modules:
  0.0 78.2 jit_solution(8142555635357521649)
XLA Ops:
  1.3 28.5 %front.1 = (bf16[6144,512]{1,0:T(8,128)(2,1)}, bf16[512,256]{1,0:T(8,128)(2,1)}, f32[24,256]{1,0:T(8,128)}, bf16[4,8,24,256]{3,2,1,0:T(8,128)(2,1)}, bf16[8,4,24...) custom-call(s32[1]{0:T(128)S(6)} %copy.15.len_ref, ...), custom_call_target="tpu_custom_call" | custom-call | tf_op jit(solution)/shard_map/front/pallas_call | solution.py:313
  29.8 45.0 %back.1 = (bf16[24,1024]{1,0:T(8,128)(2,1)}, bf16[6144,256]{1,0:T(8,128)(2,1)}, f32[128,512]{1,0:T(8,128)}, f32[64,256]{1,0:T(8,128)}, f32[64,1024]{1,0:T(8,128)...) custom-call(s32[1]{0:T(128)S(6)} %copy.15.len_ref, s32[4,8,128]{2,1,0:T(8,128)} %get-tuple-element.30.lens_ref, ...), custom_call_target="tpu_custom_call" | custom-call | tf_op jit(solution)/shard_map/back/pallas_call | solution.py:829
  74.8 3.4 %hand.1 = (bf16[24,1024]{1,0:T(8,128)(2,1)}, bf16[6144,256]{1,0:T(8,128)(2,1)}, f32[128,512]{1,0:T(8,128)}, f32[64,256]{1,0:T(8,128)}, f32[64,1024]{1,0:T(8,128)...) custom-call(bf16[24,1024]{1,0:T(8,128)(2,1)} %get-tuple-element.39.refs_0_, bf16[6144,256]{1,0:T(8,128)(2,1)} %get-tuple-element.40.refs_1_, ...), custom_call_target="tpu_custom_call" | custom-call | tf_op jit(solution)/shard_map/hand/pallas_call | solution.py:932
